TPU v7x, 32 devices: a whole 2x2x4 slice. The times are simulated.
32 devices in a mesh: dp: 16 (over z, x, core), seq: 2 (over y).
Axes of the slice: x: 2, y: 2, z: 4, core: 2. Of those that a mesh axis runs over, the one named last changes fastest.
Arguments:
- inputs: bfloat16 [32768, 768], P(('dp', 'seq')), may hold values from -6 to 6
- query_weight: bfloat16 [768, 768], P(('dp', 'seq')), may hold values from -0.21875 to 0.21875
- query_bias: bfloat16 [768], P(('dp', 'seq')), may hold values from -3 to 3
- key_weight: bfloat16 [768, 768], P(('dp', 'seq')), may hold values from -0.21875 to 0.21875
- value_weight: bfloat16 [768, 768], P(('dp', 'seq')), may hold values from -0.21875 to 0.21875
- value_bias: bfloat16 [768], P(('dp', 'seq')), may hold values from -3 to 3
- output_weight: bfloat16 [768, 768], P(('dp', 'seq')), may hold values from -1.75 to 1.75
- output_bias: bfloat16 [768], P(('dp', 'seq')), may hold values from -3 to 3
- first_gain: bfloat16 [768], P(('dp', 'seq')), may hold values from 0.5 to 1.5
- first_shift: bfloat16 [768], P(('dp', 'seq')), may hold values from -3 to 3
- inner_weight: bfloat16 [768, 3072], P(('dp', 'seq')), may hold values from -0.21875 to 0.21875
- inner_bias: bfloat16 [3072], P(('dp', 'seq')), may hold values from -3 to 3
- outer_weight: bfloat16 [3072, 768], P(('dp', 'seq')), may hold values from -0.109375 to 0.109375
- outer_bias: bfloat16 [768], P(('dp', 'seq')), may hold values from -3 to 3
- second_gain: bfloat16 [768], P(('dp', 'seq')), may hold values from 0.5 to 1.5
- second_shift: bfloat16 [768], P(('dp', 'seq')), may hold values from -3 to 3
- cotangent: bfloat16 [32768, 768], P(('dp', 'seq')), may hold values from -6 to 6
- piece_start: int32 [16, 2], P('dp'), may hold values from 0 to 1792, as said below
- memory_pos: int32 [16, 20], P('dp'), may hold values from 0 to 2047, as said below
Outputs:
- layer_out: bfloat16 [32768, 768], P(('dp', 'seq'))
- grad_inputs: float32 [32768, 768], P(('dp', 'seq'))
- grad_query_weight: float32 [768, 768], P(('dp', 'seq'))
- grad_query_bias: float32 [768], P(('dp', 'seq'))
- grad_key_weight: float32 [768, 768], P(('dp', 'seq'))
- grad_value_weight: float32 [768, 768], P(('dp', 'seq'))
- grad_value_bias: float32 [768], P(('dp', 'seq'))
- grad_output_weight: float32 [768, 768], P(('dp', 'seq'))
- grad_output_bias: float32 [768], P(('dp', 'seq'))
- grad_first_gain: float32 [768], P(('dp', 'seq'))
- grad_first_shift: float32 [768], P(('dp', 'seq'))
- grad_inner_weight: float32 [768, 3072], P(('dp', 'seq'))
- grad_inner_bias: float32 [3072], P(('dp', 'seq'))
- grad_outer_weight: float32 [3072, 768], P(('dp', 'seq'))
- grad_outer_bias: float32 [768], P(('dp', 'seq'))
- grad_second_gain: float32 [768], P(('dp', 'seq'))
- grad_second_shift: float32 [768], P(('dp', 'seq'))
Inputs may be any that keep to these rules, and one draw needn't show every extreme that they name: `piece_start`: in each sequence the 2 pieces, each of 256 positions, are in ascending order and do not intersect. `memory_pos`: the 20 positions of a sequence are distinct; the first 10 are read memory rows, the last 10 write memory rows.
All inputs are finite; a program needn't handle non-finite values.
Results may differ from a plain program's by a relative error of at most 0.035.
Values may be sent and summed in bfloat16 or wider, within the bound.
No kernel may reach another device: no remote copies, remote signals or barrier semaphores. Data moves between devices by JAX's collectives and lax.ppermute only.
A program may use at most 256 MiB of HBM per device.

v0:
```python
from functools import partial

import jax
import jax.numpy as jnp
from jax import lax
from jax.experimental import pallas as pl
from jax.experimental.pallas import tpu as pltpu
from jax.sharding import PartitionSpec as P


H = 12
HD = 64
LEN = 2048
PIC = 256
NPIC = 2
MEM = 10


norm_epsilon = 1e-05
masked_score = -1e30


def normalize(values, gain, shift):
    centre = jnp.mean(values, -1, keepdims=True)
    centred = values - centre
    spread = jnp.mean(centred * centred, -1, keepdims=True)
    return centred * lax.rsqrt(spread + norm_epsilon) * gain + shift


def gelu_exact(values):
    return jax.nn.gelu(values, approximate=False)


def visible_cols(positions, columns, starts, memories):
    labels = jnp.arange(NPIC, dtype=jnp.int32)[:, None] + 1
    in_cols = (columns[None, :] >= starts[:, None]) & (columns[None, :] < starts[:, None] + PIC)
    in_rows = (positions[None, :] >= starts[:, None]) & (positions[None, :] < starts[:, None] + PIC)
    piece_cols = jnp.sum(jnp.where(in_cols, labels, 0), 0)
    piece_rows = jnp.sum(jnp.where(in_rows, labels, 0), 0)
    same_piece = (piece_rows[:, None] == piece_cols[None, :]) & (piece_rows[:, None] > 0)
    read_cols = jnp.any(columns[None, :] == memories[:MEM, None], 0)
    write_rows = jnp.any(positions[None, :] == memories[MEM:, None], 0)
    causal = columns[None, :] <= positions[:, None]
    return causal | same_piece | read_cols[None, :] | write_rows[:, None]


def visible(positions, starts, memories):
    return visible_cols(positions, jnp.arange(LEN, dtype=jnp.int32), starts, memories)


def dense(left, right):
    return jnp.dot(left, right, preferred_element_type=jnp.float32)


def outer_product(left, right):
    return jnp.einsum("ta,tb->ab", left, right, preferred_element_type=jnp.float32)


def back_product(gradient, weight):
    return jnp.einsum("tb,ab->ta", gradient, weight, preferred_element_type=jnp.float32)


def body(
    inputs,
    query_weight,
    query_bias,
    key_weight,
    value_weight,
    value_bias,
    output_weight,
    output_bias,
    first_gain,
    first_shift,
    inner_weight,
    inner_bias,
    outer_weight,
    outer_bias,
    second_gain,
    second_shift,
    cotangent,
    piece_start,
    memory_pos,
):
    shards = (
        query_weight,
        key_weight,
        value_weight,
        output_weight,
        inner_weight,
        outer_weight,
        query_bias,
        value_bias,
        output_bias,
        first_gain,
        first_shift,
        inner_bias,
        outer_bias,
        second_gain,
        second_shift,
    )
    gathered = (
        lax.all_gather(shards[0], ("dp", "seq"), axis=0, tiled=True),
        lax.all_gather(shards[1], ("dp", "seq"), axis=0, tiled=True),
        lax.all_gather(shards[2], ("dp", "seq"), axis=0, tiled=True),
        lax.all_gather(shards[3], ("dp", "seq"), axis=0, tiled=True),
        lax.all_gather(shards[4], ("dp", "seq"), axis=0, tiled=True),
        lax.all_gather(shards[5], ("dp", "seq"), axis=0, tiled=True),
        lax.all_gather(shards[6], ("dp", "seq"), axis=0, tiled=True),
        lax.all_gather(shards[7], ("dp", "seq"), axis=0, tiled=True),
        lax.all_gather(shards[8], ("dp", "seq"), axis=0, tiled=True),
        lax.all_gather(shards[9], ("dp", "seq"), axis=0, tiled=True),
        lax.all_gather(shards[10], ("dp", "seq"), axis=0, tiled=True),
        lax.all_gather(shards[11], ("dp", "seq"), axis=0, tiled=True),
        lax.all_gather(shards[12], ("dp", "seq"), axis=0, tiled=True),
        lax.all_gather(shards[13], ("dp", "seq"), axis=0, tiled=True),
        lax.all_gather(shards[14], ("dp", "seq"), axis=0, tiled=True),
    )
    w_query, w_key, w_value, w_output, w_inner, w_outer = gathered[:6]
    vectors = [vector.astype(jnp.float32) for vector in gathered[6:]]
    b_query, b_value, b_output, g_first, s_first, b_inner, b_outer, g_second, s_second = vectors
    local_rows = inputs.shape[0]
    model_width = inputs.shape[1]
    score_scale = HD ** (-0.5)
    pair_count = H // 2
    pair_width = 2 * HD
    block_rows = min(512, local_rows, LEN)
    block_count = local_rows // block_rows
    first_row = lax.axis_index("seq") * local_rows
    query_low = (dense(inputs, w_query) + b_query).astype(jnp.bfloat16)
    key_low = dense(inputs, w_key).astype(jnp.bfloat16)
    value_low = (dense(inputs, w_value) + b_value).astype(jnp.bfloat16)
    group_keys, group_values = (
        lax.all_gather(key_low, "seq", axis=0, tiled=True),
        lax.all_gather(value_low, "seq", axis=0, tiled=True),
    )
    group_rows = group_keys.shape[0]

    def context(block_index):
        row_start = first_row + block_index * block_rows
        seq_index = row_start // LEN
        positions = row_start - seq_index * LEN + jnp.arange(block_rows, dtype=jnp.int32)
        starts = piece_start[0]
        memories = memory_pos[0]
        allowed = visible(positions, starts, memories)
        return (seq_index, allowed, group_keys, group_values)

    def pair_part(matrix, pair_index, count):
        return lax.dynamic_slice_in_dim(matrix, pair_index * pair_width, pair_width, 1).reshape(
            count, 2, HD
        )

    def pair_scores(query_pair, key_pair, allowed):
        raw = (
            jnp.einsum("qhd,khd->hqk", query_pair, key_pair, preferred_element_type=jnp.float32)
            * score_scale
        )
        return jnp.where(allowed[None], raw, masked_score)

    def forward_block(block_index):
        _, allowed, seq_keys, seq_values = context(block_index)
        block_query = lax.dynamic_slice_in_dim(query_low, block_index * block_rows, block_rows, 0)

        def forward_pair_step(carry, pair_index):
            out_buffer, total_buffer = carry
            query_pair = pair_part(block_query, pair_index, block_rows)
            key_pair = pair_part(seq_keys, pair_index, LEN)
            value_pair = pair_part(seq_values, pair_index, LEN)
            scores = pair_scores(query_pair, key_pair, allowed)
            peak = jnp.max(scores, -1, keepdims=True)
            expo_terms = jnp.exp(scores - peak)
            row_sum = jnp.sum(expo_terms, -1, keepdims=True)
            chances_low = (expo_terms / row_sum).astype(jnp.bfloat16)
            blended = jnp.einsum(
                "hqk,khd->qhd", chances_low, value_pair, preferred_element_type=jnp.float32
            )
            blended = blended.reshape(block_rows, pair_width).astype(jnp.bfloat16)
            out_buffer = lax.dynamic_update_slice_in_dim(
                out_buffer, blended, pair_index * pair_width, 1
            )
            log_pair = (peak + jnp.log(row_sum))[:, :, 0]
            total_buffer = lax.dynamic_update_slice_in_dim(
                total_buffer, log_pair, pair_index * 2, 0
            )
            return ((out_buffer, total_buffer), None)

        initial = (
            jnp.zeros((block_rows, model_width), jnp.bfloat16),
            jnp.zeros((H, block_rows), jnp.float32),
        )
        (out_buffer, total_buffer), unused = lax.scan(
            forward_pair_step, initial, jnp.arange(pair_count)
        )
        return (out_buffer, total_buffer)

    attended_blocks, log_totals = lax.map(forward_block, jnp.arange(block_count))
    attended = attended_blocks.reshape(local_rows, model_width)
    mixed = inputs.astype(jnp.float32) + dense(attended, w_output) + b_output
    hidden_norm, first_pull = jax.vjp(normalize, mixed, g_first, s_first)
    hidden_low = hidden_norm.astype(jnp.bfloat16)
    inner = dense(hidden_low, w_inner) + b_inner
    activated_full, gelu_pull = jax.vjp(gelu_exact, inner)
    activated = activated_full.astype(jnp.bfloat16)
    second_in = hidden_norm + dense(activated, w_outer) + b_outer
    normed_out, second_pull = jax.vjp(normalize, second_in, g_second, s_second)
    layer_out = normed_out.astype(jnp.bfloat16)
    back_weights = (
        lax.all_gather(query_weight, ("dp", "seq"), axis=0, tiled=True),
        lax.all_gather(key_weight, ("dp", "seq"), axis=0, tiled=True),
        lax.all_gather(value_weight, ("dp", "seq"), axis=0, tiled=True),
        lax.all_gather(output_weight, ("dp", "seq"), axis=0, tiled=True),
        lax.all_gather(inner_weight, ("dp", "seq"), axis=0, tiled=True),
        lax.all_gather(outer_weight, ("dp", "seq"), axis=0, tiled=True),
    )
    v_query, v_key, v_value, v_output, v_inner, v_outer = back_weights
    grad_second_in, grad_second_gain, grad_second_shift = second_pull(cotangent.astype(jnp.float32))
    grad_outer_bias = jnp.sum(grad_second_in, 0)
    second_low = grad_second_in.astype(jnp.bfloat16)
    grad_outer_weight = outer_product(activated, second_low)
    (grad_inner,) = gelu_pull(back_product(second_low, v_outer))
    grad_inner_bias = jnp.sum(grad_inner, 0)
    inner_low = grad_inner.astype(jnp.bfloat16)
    grad_inner_weight = outer_product(hidden_low, inner_low)
    grad_hidden = grad_second_in + back_product(inner_low, v_inner)
    grad_mixed, grad_first_gain, grad_first_shift = first_pull(grad_hidden)
    grad_output_bias = jnp.sum(grad_mixed, 0)
    mixed_low = grad_mixed.astype(jnp.bfloat16)
    grad_output_weight = outer_product(attended, mixed_low)
    grad_attended = back_product(mixed_low, v_output).astype(jnp.bfloat16)

    def backward_block(carry, block_index):
        _, allowed, seq_keys, seq_values = context(block_index)
        block_query = lax.dynamic_slice_in_dim(query_low, block_index * block_rows, block_rows, 0)
        block_grad = lax.dynamic_slice_in_dim(
            grad_attended, block_index * block_rows, block_rows, 0
        )
        block_total = log_totals[block_index]

        def backward_pair_step(inner_carry, pair_index):
            query_grad, term_buffer = (inner_carry[0], inner_carry[1])
            query_pair = pair_part(block_query, pair_index, block_rows)
            key_pair = pair_part(seq_keys, pair_index, LEN)
            value_pair = pair_part(seq_values, pair_index, LEN)
            grad_pair = pair_part(block_grad, pair_index, block_rows)
            scores = pair_scores(query_pair, key_pair, allowed)
            total_pair = lax.dynamic_slice_in_dim(block_total, pair_index * 2, 2, 0)
            chances = jnp.exp(scores - total_pair[:, :, None])
            chance_grad = jnp.einsum(
                "qhd,khd->hqk", grad_pair, value_pair, preferred_element_type=jnp.float32
            )
            row_terms = jnp.sum(chances * chance_grad, -1, keepdims=True)
            score_grad = (chances * (chance_grad - row_terms)).astype(jnp.bfloat16)
            query_part = jnp.einsum(
                "hqk,khd->qhd", score_grad, key_pair, preferred_element_type=jnp.float32
            )
            query_part = query_part.reshape(block_rows, pair_width) * score_scale
            query_grad = lax.dynamic_update_slice_in_dim(
                query_grad, query_part, pair_index * pair_width, 1
            )
            term_buffer = lax.dynamic_update_slice_in_dim(
                term_buffer, row_terms[:, :, 0], pair_index * 2, 0
            )
            seq_key_grad, seq_value_grad = (inner_carry[2], inner_carry[3])
            chances_low = chances.astype(jnp.bfloat16)
            key_part = jnp.einsum(
                "hqk,qhd->khd", score_grad, query_pair, preferred_element_type=jnp.float32
            )
            value_part = jnp.einsum(
                "hqk,qhd->khd", chances_low, grad_pair, preferred_element_type=jnp.float32
            )
            key_part = key_part.reshape(LEN, pair_width) * score_scale
            value_part = value_part.reshape(LEN, pair_width)
            seq_key_grad = lax.dynamic_update_slice_in_dim(
                seq_key_grad, key_part, pair_index * pair_width, 1
            )
            seq_value_grad = lax.dynamic_update_slice_in_dim(
                seq_value_grad, value_part, pair_index * pair_width, 1
            )
            return ((query_grad, term_buffer, seq_key_grad, seq_value_grad), None)

        initial = (
            jnp.zeros((block_rows, model_width), jnp.float32),
            jnp.zeros((H, block_rows), jnp.float32),
        )
        initial = initial + (
            jnp.zeros((LEN, model_width), jnp.float32),
            jnp.zeros((LEN, model_width), jnp.float32),
        )
        finals, _ = lax.scan(backward_pair_step, initial, jnp.arange(pair_count))
        key_grads, value_grads = carry
        key_grads = key_grads + finals[2]
        value_grads = value_grads + finals[3]
        carry = (key_grads, value_grads)
        return (carry, (finals[0], finals[1]))

    group_zero = jnp.zeros((group_rows, model_width), jnp.float32)
    (key_grads, value_grads), (query_blocks, term_blocks) = lax.scan(
        backward_block, (group_zero, group_zero), jnp.arange(block_count)
    )
    key_sum, value_sum = (
        lax.psum_scatter(
            key_grads.astype(jnp.bfloat16), "seq", scatter_dimension=0, tiled=True
        ).astype(jnp.float32),
        lax.psum_scatter(
            value_grads.astype(jnp.bfloat16), "seq", scatter_dimension=0, tiled=True
        ).astype(jnp.float32),
    )
    query_sum = query_blocks.reshape(local_rows, model_width)
    grad_query_bias = jnp.sum(query_sum, 0)
    grad_value_bias = jnp.sum(value_sum, 0)
    query_grad_low = query_sum.astype(jnp.bfloat16)
    key_grad_low = key_sum.astype(jnp.bfloat16)
    value_grad_low = value_sum.astype(jnp.bfloat16)
    grad_query_weight = outer_product(inputs, query_grad_low)
    grad_key_weight = outer_product(inputs, key_grad_low)
    grad_value_weight = outer_product(inputs, value_grad_low)
    grad_inputs = (
        grad_mixed
        + back_product(query_grad_low, v_query)
        + back_product(key_grad_low, v_key)
        + back_product(value_grad_low, v_value)
    )
    grads = (
        grad_query_weight,
        grad_key_weight,
        grad_value_weight,
        grad_output_weight,
        grad_inner_weight,
        grad_outer_weight,
        grad_query_bias,
        grad_value_bias,
        grad_output_bias,
        grad_first_gain,
        grad_first_shift,
        grad_inner_bias,
        grad_outer_bias,
        grad_second_gain,
        grad_second_shift,
    )
    owned = (
        lax.psum_scatter(grads[0], ("dp", "seq"), scatter_dimension=0, tiled=True),
        lax.psum_scatter(grads[1], ("dp", "seq"), scatter_dimension=0, tiled=True),
        lax.psum_scatter(grads[2], ("dp", "seq"), scatter_dimension=0, tiled=True),
        lax.psum_scatter(grads[3], ("dp", "seq"), scatter_dimension=0, tiled=True),
        lax.psum_scatter(grads[4], ("dp", "seq"), scatter_dimension=0, tiled=True),
        lax.psum_scatter(grads[5], ("dp", "seq"), scatter_dimension=0, tiled=True),
        lax.psum_scatter(grads[6], ("dp", "seq"), scatter_dimension=0, tiled=True),
        lax.psum_scatter(grads[7], ("dp", "seq"), scatter_dimension=0, tiled=True),
        lax.psum_scatter(grads[8], ("dp", "seq"), scatter_dimension=0, tiled=True),
        lax.psum_scatter(grads[9], ("dp", "seq"), scatter_dimension=0, tiled=True),
        lax.psum_scatter(grads[10], ("dp", "seq"), scatter_dimension=0, tiled=True),
        lax.psum_scatter(grads[11], ("dp", "seq"), scatter_dimension=0, tiled=True),
        lax.psum_scatter(grads[12], ("dp", "seq"), scatter_dimension=0, tiled=True),
        lax.psum_scatter(grads[13], ("dp", "seq"), scatter_dimension=0, tiled=True),
        lax.psum_scatter(grads[14], ("dp", "seq"), scatter_dimension=0, tiled=True),
    )
    return (
        layer_out,
        grad_inputs,
        owned[0],
        owned[6],
        owned[1],
        owned[2],
        owned[7],
        owned[3],
        owned[8],
        owned[9],
        owned[10],
        owned[4],
        owned[11],
        owned[5],
        owned[12],
        owned[13],
        owned[14],
    )


F32=jnp.float32; BF=jnp.bfloat16
NT=(((1,),(1,)),((),()))
NN=(((1,),(0,)),((),()))


def mm(a,b,dims=NN):
    return lax.dot_general(a,b,dims,preferred_element_type=F32)


GROUP=16


def half_mask(shape, head, dim):
    lanes=lax.broadcasted_iota(jnp.int32,shape,dim)
    return (lanes<64) if head==0 else (lanes>=64)


def only(x, head):
    return jnp.where(half_mask(x.shape,head,1),x,jnp.zeros_like(x))


def take_rows(ref, pos_ref, first):
    width=ref.shape[1]
    out=jnp.zeros((GROUP,width),F32)
    rows=lax.broadcasted_iota(jnp.int32,(GROUP,width),0)
    for m in range(MEM):
        pos=pos_ref[first+m]
        start=pl.multiple_of((pos//GROUP)*GROUP,GROUP)
        part=ref[pl.ds(start,GROUP),:].astype(F32)
        row=jnp.sum(jnp.where(rows==pos-start,part,0.0),0,keepdims=True)
        out=jnp.where(rows==m,row,out)
    return out.astype(BF)


def put_rows(ref, pos_ref, first, values, add):
    width=ref.shape[1]
    rows=lax.broadcasted_iota(jnp.int32,(GROUP,width),0)
    for m in range(MEM):
        pos=pos_ref[first+m]
        start=pl.multiple_of((pos//GROUP)*GROUP,GROUP)
        old=ref[pl.ds(start,GROUP),:].astype(F32)
        row=values[m:m+1,:]
        new=jnp.where(rows==pos-start,old+row if add else row,old)
        ref[pl.ds(start,GROUP),:]=new.astype(ref.dtype)


def transposed(x):
    return jnp.transpose(x.astype(F32)).astype(BF)


def fwd_kernel(pos_ref, posv_ref, limit_ref, write_ref, qkv_ref, o_ref, lse_ref, vt_ref, qt_ref, acc_ref, *, bq, np_, qb0, qb1):
    rows_all=qkv_ref.shape[0]
    nq=rows_all//bq
    W=np_*128
    nh=2*np_
    cols=lambda part,p:slice(part*W+p*128,part*W+p*128+128)
    hr=lambda h:slice(80*h,80*h+80)
    mem=take_rows(qkv_ref,pos_ref,0)
    kr=[only(mem[:,cols(1,h//2)],h%2) for h in range(nh)]
    ones16=jnp.ones((16,GROUP),BF)
    vrt=[]
    for p in range(np_):
        vt=transposed(qkv_ref[:,cols(2,p)])
        mt=transposed(mem[:,cols(2,p)])
        qt_ref[p*128:p*128+128,:]=transposed(qkv_ref[:,cols(0,p)])
        for h in range(2):
            vt_ref[80*(2*p+h):80*(2*p+h)+64,:]=vt[64*h:64*h+64]
            vt_ref[80*(2*p+h)+64:80*(2*p+h)+80,:]=jnp.ones((16,rows_all),BF)
            vrt.append(jnp.concatenate([mt[64*h:64*h+64],ones16],0))
    read_pos=posv_ref[...]
    def q_step(qb, unused):
        q0=pl.multiple_of(qb*bq,bq)
        limit=limit_ref[:,pl.ds(q0,bq)][0:1]
        key_iota=lax.broadcasted_iota(jnp.int32,(bq,bq),0)
        zq=jnp.zeros((64,bq),BF)
        def qh(h):
            own=qt_ref[64*h:64*h+64,pl.ds(q0,bq)]
            return jnp.concatenate([own,zq] if h%2==0 else [zq,own],0)
        def soft(h,s,vt,m):
            m2=jnp.maximum(m,jnp.max(s,0,keepdims=True))
            fix=jnp.exp2(m-m2)
            p=jnp.exp2(s-m2)
            acc_ref[hr(h),:]=acc_ref[hr(h),:]*fix+mm(vt,p.astype(BF))
            return m2
        def block(kb,carry,mask):
            k0=pl.multiple_of(kb*bq,bq)
            ss=[mm(qkv_ref[pl.ds(k0,bq),cols(1,h//2)],qh(h)) for h in range(nh)]
            if mask:
                ss=[jnp.where(key_iota+k0<=limit,s,masked_score) for s in ss]
            return tuple(soft(h,ss[h],vt_ref[hr(h),pl.ds(k0,bq)],carry[h]) for h in range(nh))
        acc_ref[...]=jnp.zeros_like(acc_ref)
        carry=tuple(jnp.full((1,bq),masked_score,F32) for _ in range(nh))
        carry=block(qb,carry,True)
        carry=tuple(soft(h,jnp.where(read_pos>limit,mm(kr[h],qh(h)),masked_score),vrt[h],carry[h]) for h in range(nh))
        carry=lax.fori_loop(0,qb,lambda kb,c:block(kb,c,False),carry)
        far=jnp.max(limit)>=q0+bq
        carry=lax.cond(far,lambda c:block(jnp.minimum(qb+1,nq-1),c,True),lambda c:c,carry)
        wr=write_ref[:,pl.ds(q0,bq)][0:1]
        outs=[]
        for h in range(nh):
            l=acc_ref[80*h+64:80*h+65,:]
            outs.append(acc_ref[80*h:80*h+64,:]/l)
            lse=carry[h]+jnp.log2(l)
            lse_ref[h:h+1,pl.ds(q0,bq)]=jnp.where(wr>0,1e30,lse)
        o_ref[pl.ds(q0,bq),:]=jnp.transpose(jnp.concatenate(outs,0)).astype(BF)
        return unused
    lax.fori_loop(qb0,qb1,q_step,0)
    rows=take_rows(qkv_ref,pos_ref,MEM)
    out=[]
    for p in range(np_):
        total=jnp.zeros((GROUP,128),F32)
        qw=rows[:,cols(0,p)]
        for h in range(2):
            s=mm(only(qw,h),qkv_ref[:,cols(1,p)],NT)
            m=jnp.max(s,1,keepdims=True)
            e=jnp.exp2(s-m)
            l=jnp.sum(e,1,keepdims=True)
            ow=mm(e.astype(BF),qkv_ref[:,cols(2,p)])/l
            total=total+jnp.where(half_mask((GROUP,128),h,1),ow,0.0)
        out.append(total)
    put_rows(o_ref,pos_ref,MEM,jnp.concatenate(out,1),False)


LN2=0.6931471805599453


def bwd_kernel(pos_ref, posv_ref, limit_ref, qkv_ref, do_ref, o_ref, lse_ref,
               dqkv_ref, bias_ref, qt_ref, kt_ref, dot_ref, dk_acc, dv_acc, dq_acc, dr_acc, *, bq, scale, np_):
    rows_all=qkv_ref.shape[0]
    nq=rows_all//bq
    W=np_*128
    nh=2*np_
    cols=lambda part,p:slice(part*W+p*128,part*W+p*128+128)
    pc=lambda p:slice(p*128,p*128+128)
    hr=lambda h:slice(64*h,64*h+64)
    for p in range(np_):
        qt_ref[pc(p),:]=transposed(qkv_ref[:,cols(0,p)])
        kt_ref[pc(p),:]=transposed(qkv_ref[:,cols(1,p)])
        dot_ref[pc(p),:]=transposed(do_ref[:,pc(p)])
    mem=take_rows(qkv_ref,pos_ref,0)
    kr=[mem[:,cols(1,p)] for p in range(np_)]
    vr=[mem[:,cols(2,p)] for p in range(np_)]
    krt=[transposed(kr[p]) for p in range(np_)]
    read_pos=posv_ref[...]
    rows=take_rows(qkv_ref,pos_ref,MEM)
    dow_all=take_rows(do_ref,pos_ref,MEM)
    valid=lax.broadcasted_iota(jnp.int32,(GROUP,1),0)<MEM
    dqw_all=[]
    for pr in range(np_):
        qw=rows[:,cols(0,pr)]
        dow=dow_all[:,pc(pr)]
        qwt=transposed(qw); dowt=transposed(dow)
        dqw=jnp.zeros((GROUP,128),F32)
        for h in range(2):
            s=mm(only(qw,h),qkv_ref[:,cols(1,pr)],NT)
            m=jnp.max(s,1,keepdims=True)
            p=jnp.exp2(s-m)
            p=p*jnp.where(valid,1.0/jnp.sum(p,1,keepdims=True),0.0)
            dp=mm(only(dow,h),qkv_ref[:,cols(2,pr)],NT)
            ds=(p*(dp-jnp.sum(p*dp,1,keepdims=True))).astype(BF)
            dqw=dqw+jnp.where(half_mask((GROUP,128),h,1),mm(ds,qkv_ref[:,cols(1,pr)]),0.0)
            dk_acc[hr(2*pr+h),:]=mm(qwt[64*h:64*h+64],ds)
            dv_acc[hr(2*pr+h),:]=mm(dowt[64*h:64*h+64],p.astype(BF))
        dqw_all.append(dqw)
    dr_acc[...]=jnp.zeros_like(dr_acc)
    def q_step(qb, unused):
        q0=pl.multiple_of(qb*bq,bq)
        limit=limit_ref[:,pl.ds(q0,bq)][0:1]
        zq=jnp.zeros((64,bq),BF)
        def padded(ref,h):
            own=ref[hr(h),pl.ds(q0,bq)]
            return jnp.concatenate([own,zq] if h%2==0 else [zq,own],0)
        prod=jnp.transpose(do_ref[pl.ds(q0,bq),:].astype(F32)*o_ref[pl.ds(q0,bq),:].astype(F32))
        delta=[jnp.sum(prod[hr(h)],0,keepdims=True) for h in range(nh)]
        lse=[lse_ref[h:h+1,pl.ds(q0,bq)] for h in range(nh)]
        key_iota=lax.broadcasted_iota(jnp.int32,(bq,bq),0)
        dq_acc[...]=jnp.zeros_like(dq_acc)
        def grads(h,s,v):
            p=jnp.exp2(s-lse[h])
            dp=mm(v,padded(dot_ref,h))
            return (p*(dp-delta[h])).astype(BF),p.astype(BF)
        def block(kb,mask):
            k0=pl.multiple_of(kb*bq,bq)
            ks=pl.ds(k0,bq)
            held={}
            def front(h):
                s=mm(qkv_ref[ks,cols(1,h//2)],padded(qt_ref,h))
                if mask:
                    s=jnp.where(key_iota+k0<=limit,s,masked_score)
                held[h]=(s,mm(qkv_ref[ks,cols(2,h//2)],padded(dot_ref,h)))
            def middle(h):
                s,dp=held[h]
                p=jnp.exp2(s-lse[h])
                held[h]=((p*(dp-delta[h])).astype(BF),p.astype(BF))
            def back(h):
                ds,p=held[h]
                dq_acc[hr(h),:]+=mm(kt_ref[hr(h),ks],ds)
                dk_acc[hr(h),ks]+=mm(qt_ref[hr(h),pl.ds(q0,bq)],ds,NT)
                dv_acc[hr(h),ks]+=mm(dot_ref[hr(h),pl.ds(q0,bq)],p,NT)
            for h in range(nh+2):
                if h<nh:
                    front(h)
                if 0<=h-1<nh:
                    middle(h-1)
                if h>=2:
                    back(h-2)
        block(qb,True)
        for h in range(nh):
            s=jnp.where(read_pos>limit,mm(kr[h//2],padded(qt_ref,h)),masked_score)
            ds,p=grads(h,s,vr[h//2])
            dr_acc[0,hr(h),:]+=mm(qt_ref[hr(h),pl.ds(q0,bq)],ds,NT)
            dr_acc[1,hr(h),:]+=mm(dot_ref[hr(h),pl.ds(q0,bq)],p,NT)
            dq_acc[hr(h),:]+=mm(krt[h//2][64*(h%2):64*(h%2)+64,:],ds)
        def step(kb,c):
            block(kb,False)
            return c
        lax.fori_loop(0,qb,step,0)
        @pl.when(jnp.max(limit)>=q0+bq)
        def _():
            block(jnp.minimum(qb+1,nq-1),True)
        dqkv_ref[pl.ds(q0,bq),0:W]=(jnp.transpose(dq_acc[...])*scale).astype(BF)
        return unused
    lax.fori_loop(0,nq,q_step,0)
    put_rows(dqkv_ref.at[:,0:W],pos_ref,MEM,jnp.concatenate(dqw_all,1)*scale,False)
    for p in range(np_):
        dqkv_ref[:,cols(1,p)]=(jnp.transpose(dk_acc[pc(p),:])*LN2).astype(BF)
        dqkv_ref[:,cols(2,p)]=jnp.transpose(dv_acc[pc(p),:]).astype(BF)
    put_rows(dqkv_ref.at[:,W:2*W],pos_ref,0,jnp.transpose(dr_acc[0])*LN2,True)
    put_rows(dqkv_ref.at[:,2*W:3*W],pos_ref,0,jnp.transpose(dr_acc[1]),True)
    rows8=lax.broadcasted_iota(jnp.int32,(8,W),0)
    bq_sum=jnp.sum(dqkv_ref[:,0:W].astype(F32),0,keepdims=True)
    bv_sum=jnp.sum(dqkv_ref[:,2*W:3*W].astype(F32),0,keepdims=True)
    bias_ref[...]=jnp.where(rows8==0,bq_sum,jnp.where(rows8==1,bv_sum,0.0))


ONCE=pl.Buffered(1)


def attn_fwd(qkv, pos, posv, limit, write, np_, bq=256, qb0=0, qb1=None):
    L=qkv.shape[0]; W=np_*128
    row8=pl.BlockSpec((8,L),lambda i:(0,0),pipeline_mode=ONCE)
    full=lambda w:pl.BlockSpec((L,w),lambda i:(0,0),pipeline_mode=ONCE)
    return pl.pallas_call(partial(fwd_kernel,bq=bq,np_=np_,qb0=qb0,qb1=L//bq if qb1 is None else qb1),
        grid=(1,),
        in_specs=[pl.BlockSpec(memory_space=pltpu.SMEM),pl.BlockSpec((GROUP,1),lambda i:(0,0)),row8,row8,full(3*W)],
        out_specs=[full(W),row8],
        out_shape=[jax.ShapeDtypeStruct((L,W),BF),jax.ShapeDtypeStruct((8,L),F32)],
        scratch_shapes=[pltpu.VMEM((np_*160,L),BF),pltpu.VMEM((W,L),BF),pltpu.VMEM((np_*160,bq),F32)],
        name="attn_fwd",
    )(pos,posv,limit,write,qkv)


def attn_bwd(qkv, pos, posv, limit, do, o, lse, np_, scale, bq=256):
    L=qkv.shape[0]; W=np_*128
    row8=pl.BlockSpec((8,L),lambda i:(0,0),pipeline_mode=ONCE)
    full=lambda w:pl.BlockSpec((L,w),lambda i:(0,0),pipeline_mode=ONCE)
    return pl.pallas_call(partial(bwd_kernel,bq=bq,scale=scale,np_=np_),
        grid=(1,),
        in_specs=[pl.BlockSpec(memory_space=pltpu.SMEM),pl.BlockSpec((GROUP,1),lambda i:(0,0)),row8,full(3*W),full(W),full(W),row8],
        out_specs=[full(3*W),pl.BlockSpec((8,W),lambda i:(0,0))],
        out_shape=[jax.ShapeDtypeStruct((L,3*W),BF),jax.ShapeDtypeStruct((8,W),F32)],
        scratch_shapes=[pltpu.VMEM((W,L),BF)]*3+[pltpu.VMEM((W,L),F32)]*2+[pltpu.VMEM((W,bq),F32),pltpu.VMEM((2,W,GROUP),F32)],
        name="attn_bwd",
    )(pos,posv,limit,qkv,do,o,lse)


LOG2E = 1.4426950408889634
ALL = ("dp", "seq")
RSQRT2 = 0.7071067811865476
RSQRT2PI = 0.3989422804014327


def bit_swap(x, axis, size, bit):
    return lax.ppermute(x, axis, [(i, i ^ bit) for i in range(size)])


def side(flag, own, peer, axis):
    low = jnp.where(flag, peer, own)
    high = jnp.where(flag, own, peer)
    return jnp.concatenate([low, high], axis)


def bits_of(size):
    out = []
    bit = 1
    while bit < size:
        out.append(bit)
        bit *= 2
    return out


def gather_dp(block, size):
    bits = bits_of(size)[::-1]
    index = lax.axis_index("dp")
    out = block
    for bit in bits:
        other = bit_swap(out, "dp", size, bit)
        up = (index & bit) != 0
        out = jnp.stack([jnp.where(up, other, out), jnp.where(up, out, other)])
    count = len(bits)
    out = out.transpose(tuple(range(count))[::-1] + tuple(range(count, out.ndim)))
    return out.reshape((size,) + block.shape)


def halve_dp(rest, size, bit):
    up = (lax.axis_index("dp") & bit) != 0
    rest = rest.reshape((rest.shape[0] // 2, 2) + rest.shape[1:])
    give = jnp.where(up, rest[:, 0], rest[:, 1]).astype(BF)
    keep = jnp.where(up, rest[:, 1], rest[:, 0])
    got = bit_swap(give, "dp", size, bit)
    return keep + got.astype(F32)


def norm_parts(values):
    centre = jnp.mean(values, -1, keepdims=True)
    centred = values - centre
    spread = jnp.mean(centred * centred, -1, keepdims=True)
    factor = lax.rsqrt(spread + norm_epsilon)
    return centred * factor, factor


def norm_back(gradient, unit, factor):
    return factor * (
        gradient
        - jnp.mean(gradient, -1, keepdims=True)
        - unit * jnp.mean(gradient * unit, -1, keepdims=True)
    )


def fast_body(
    inputs,
    query_weight,
    query_bias,
    key_weight,
    value_weight,
    value_bias,
    output_weight,
    output_bias,
    first_gain,
    first_shift,
    inner_weight,
    inner_bias,
    outer_weight,
    outer_bias,
    second_gain,
    second_shift,
    cotangent,
    piece_start,
    memory_pos,
    *,
    n_dp,
):
    rows, width = inputs.shape
    inner_width = inner_weight.shape[1]
    devices = 2 * n_dp
    part = width // devices
    inner_part = inner_width // devices
    ratio = inner_width // width
    half = width // 2
    seq = lax.axis_index("seq")
    upper = seq == 1

    def swap(x):
        return bit_swap(x, "seq", 2, 1)

    wide = inner_weight.reshape(part, ratio, width).transpose(1, 0, 2).reshape(ratio * part, width)
    packed = jnp.concatenate([output_weight, wide, outer_weight], 0)
    late = lax.all_gather(packed, ALL, axis=0, tiled=False)
    peer_inputs = swap(inputs)
    vectors = jnp.concatenate(
        [
            query_bias,
            value_bias,
            output_bias,
            first_gain,
            first_shift,
            outer_bias,
            second_gain,
            second_shift,
            inner_bias,
        ]
    )
    count = vectors.shape[0]
    three = jnp.stack([query_weight, key_weight, value_weight], 1)
    three = three.reshape(part, 3, 2, half)
    line = jnp.pad(vectors, (0, 3 * half - count))[None, :]
    line = jnp.pad(line, ((0, 7), (0, 0)))

    def columns(upper_half):
        kept = jnp.where(upper_half, three[:, :, 1], three[:, :, 0]).reshape(part, 3 * half)
        return jnp.concatenate([kept, line], 0)

    pair = side(upper, columns(upper)[None], swap(columns(jnp.logical_not(upper)))[None], 0)
    early = gather_dp(pair, n_dp).reshape(devices, part + 8, 3 * half)
    w_three = early[:, :part].reshape(width, 3 * half)
    lines = early[:, part, :count].astype(F32)
    vector = lambda k: lines[:, k * part : (k + 1) * part].reshape(width)
    b_query, b_value, b_output, g_first, s_first, b_outer, g_second, s_second = map(vector, range(8))
    b_inner = lines[:, 8 * part :].reshape(inner_width)
    own_half = lambda v: jnp.where(upper, v[half:], v[:half])
    features = side(upper, inputs, peer_inputs, 0)
    scale = HD ** (-0.5)
    shift = jnp.concatenate([own_half(b_query), jnp.zeros((half,), F32), own_half(b_value)])
    grow = jnp.concatenate([jnp.full((half,), scale * LOG2E, F32), jnp.ones((2 * half,), F32)])
    qkv = ((dense(features, w_three) + shift) * grow).astype(BF)
    positions = jnp.arange(2 * rows, dtype=jnp.int32)
    limit = positions
    for piece in range(NPIC):
        start = piece_start[0, piece]
        inside = (positions >= start) & (positions < start + PIC)
        limit = jnp.where(inside, start + PIC - 1, limit)
    memories = memory_pos[0]
    writes = jnp.any(positions[None, :] == memories[MEM:, None], 0).astype(jnp.int32)
    limit = jnp.broadcast_to(limit, (8, 2 * rows))
    writes = jnp.broadcast_to(writes, (8, 2 * rows))
    reads = jnp.pad(memories[:MEM], (0, GROUP - MEM), constant_values=-1)[:, None]
    pairs = half // (2 * HD)
    out_heads, totals = attn_fwd(qkv, memories, reads, limit, writes, pairs)
    other_rows = jnp.where(upper, out_heads[:rows], out_heads[rows:])
    own_rows = jnp.where(upper, out_heads[rows:], out_heads[:rows])
    attended = side(upper, own_rows, swap(other_rows), 1)
    w_output = late[:, :part].reshape(width, width)
    w_inner = jnp.concatenate(
        [
            late[:, part + k * part : 2 * part + k * part].reshape(width, width)
            for k in range(ratio)
        ],
        1,
    )
    w_outer = late[:, part + ratio * part :].reshape(inner_width, width)
    mixed = inputs.astype(F32) + dense(attended, w_output) + b_output
    first_unit, first_factor = norm_parts(mixed)
    hidden_norm = first_unit * g_first + s_first
    hidden_low = hidden_norm.astype(BF)
    inner = dense(hidden_low, w_inner) + b_inner
    chance = 0.5 * (1.0 + lax.erf(inner * RSQRT2))
    activated = (inner * chance).astype(BF)
    slope = (chance + inner * (RSQRT2PI * jnp.exp(-0.5 * inner * inner))).astype(BF)
    activated, slope = lax.optimization_barrier((activated, slope))
    second_in = hidden_norm + dense(activated, w_outer) + b_outer
    second_unit, second_factor = norm_parts(second_in)
    layer_out = (second_unit * g_second + s_second).astype(BF)
    cot = cotangent.astype(F32)
    grad_second_gain = jnp.sum(cot * second_unit, 0)
    grad_second_shift = jnp.sum(cot, 0)
    grad_second_in = norm_back(cot * g_second, second_unit, second_factor)
    grad_outer_bias = jnp.sum(grad_second_in, 0)
    second_low = grad_second_in.astype(BF)
    grad_inner = back_product(second_low, w_outer) * slope.astype(F32)
    grad_inner_bias = jnp.sum(grad_inner, 0)
    inner_low = grad_inner.astype(BF)
    column = lambda k: inner_low[:, k * width : (k + 1) * width]
    inner_blocks = [
        outer_product(hidden_low, column(k)).astype(BF).reshape(devices, part, width)
        for k in range(ratio)
    ]
    grad_outer_weight = outer_product(activated, second_low).astype(BF)
    bundle = jnp.concatenate(
        inner_blocks + [grad_outer_weight.reshape(devices, inner_part, width)], 1
    )
    bundle_rows = bundle.shape[1]
    bundle, inner_low = lax.optimization_barrier((bundle, inner_low))
    reduced = lax.psum_scatter(
        bundle.reshape(devices * bundle_rows, width), ALL, scatter_dimension=0, tiled=True
    )
    grad_hidden = grad_second_in + back_product(inner_low, w_inner)
    grad_first_gain = jnp.sum(grad_hidden * first_unit, 0)
    grad_first_shift = jnp.sum(grad_hidden, 0)
    grad_mixed = norm_back(grad_hidden * g_first, first_unit, first_factor)
    grad_output_bias = jnp.sum(grad_mixed, 0)
    mixed_low = grad_mixed.astype(BF)
    grad_attended = back_product(mixed_low, w_output).astype(BF)
    grad_other = jnp.where(upper, grad_attended[:, :half], grad_attended[:, half:])
    grad_own = jnp.where(upper, grad_attended[:, half:], grad_attended[:, :half])
    grad_heads = side(upper, grad_own, swap(grad_other), 0)
    grad_output_weight = outer_product(attended, mixed_low).reshape(devices, part, width)
    thin = [
        grad_output_bias,
        grad_first_gain,
        grad_first_shift,
        grad_outer_bias,
        grad_second_gain,
        grad_second_shift,
    ]
    thin = jnp.concatenate(
        [v.reshape(devices, part) for v in thin] + [grad_inner_bias.reshape(devices, inner_part)], 1
    )
    thin = jnp.pad(thin[:, None, :], ((0, 0), (0, 7), (0, width - thin.shape[1])))
    mid = jnp.concatenate([grad_output_weight, thin], 1).reshape(n_dp, 2, part + 8, width)
    bits = bits_of(n_dp)
    mid = halve_dp(mid, n_dp, bits[0])
    grads, bias_sums = attn_bwd(
        qkv, memories, reads, limit, grad_heads, out_heads, totals, pairs, scale
    )
    other_grads = jnp.where(upper, grads[:rows], grads[rows:])
    own_grads = jnp.where(upper, grads[rows:], grads[:rows])
    for_peer = back_product(other_grads, w_three).astype(BF)
    for_peer, grads = lax.optimization_barrier((for_peer, grads))
    sent = swap(for_peer)
    three_grad = outer_product(features, grads).reshape(devices, part, 3 * half)
    full = lambda v: side(upper, v, jnp.zeros_like(v), 0).reshape(devices, part)
    tails = jnp.concatenate([full(bias_sums[0]), full(bias_sums[1])], 1)
    tails = jnp.pad(tails[:, None, :], ((0, 0), (0, 7), (0, 3 * half - 2 * part)))
    blocks = jnp.concatenate([three_grad, tails], 1).reshape(n_dp, 2, part + 8, 3 * half)
    blocks = halve_dp(blocks, n_dp, bits[0])
    own_part = lax.optimization_barrier(grad_mixed + back_product(own_grads, w_three))
    mid = halve_dp(mid, n_dp, bits[1])
    blocks = halve_dp(blocks, n_dp, bits[1])
    blocks = jnp.concatenate([blocks, mid], 3)
    for bit in bits[2:]:
        blocks = halve_dp(blocks, n_dp, bit)
    mine = blocks[0]
    give = jnp.where(upper, mine[0], mine[1])
    keep = jnp.where(upper, mine[1], mine[0])
    got = swap(give.astype(BF)).astype(F32)
    grad_inputs = own_part + sent.astype(F32)
    total = keep[:, 3 * half :] + got[:, 3 * half :]
    tail_sum = keep[part, : 2 * part] + got[part, : 2 * part]
    keep = keep[:part, : 3 * half].reshape(part, 3, half)
    got = got[:part, : 3 * half].reshape(part, 3, half)
    matrices = side(upper, keep, got, 2)
    thin_part = lambda k: total[part, k * part : (k + 1) * part]
    reduced = reduced.astype(F32)
    own_inner = jnp.concatenate([reduced[k * part : (k + 1) * part] for k in range(ratio)], 1)
    own_outer = reduced[ratio * part :]
    return (
        layer_out,
        grad_inputs,
        matrices[:, 0],
        tail_sum[:part],
        matrices[:, 1],
        matrices[:, 2],
        tail_sum[part:],
        total[:part],
        thin_part(0),
        thin_part(1),
        thin_part(2),
        own_inner,
        total[part, 6 * part : 6 * part + inner_part],
        own_outer,
        thin_part(3),
        thin_part(4),
        thin_part(5),
    )


def solution(mesh):
    in_specs = (
        P(("dp", "seq"), None),
        P(("dp", "seq"), None),
        P(("dp", "seq")),
        P(("dp", "seq"), None),
        P(("dp", "seq"), None),
        P(("dp", "seq")),
        P(("dp", "seq"), None),
        P(("dp", "seq")),
        P(("dp", "seq")),
        P(("dp", "seq")),
        P(("dp", "seq"), None),
        P(("dp", "seq")),
        P(("dp", "seq"), None),
        P(("dp", "seq")),
        P(("dp", "seq")),
        P(("dp", "seq")),
        P(("dp", "seq"), None),
        P("dp", None),
        P("dp", None),
    )
    out_specs = (
        P(("dp", "seq"), None),
        P(("dp", "seq"), None),
        P(("dp", "seq"), None),
        P(("dp", "seq")),
        P(("dp", "seq"), None),
        P(("dp", "seq"), None),
        P(("dp", "seq")),
        P(("dp", "seq"), None),
        P(("dp", "seq")),
        P(("dp", "seq")),
        P(("dp", "seq")),
        P(("dp", "seq"), None),
        P(("dp", "seq")),
        P(("dp", "seq"), None),
        P(("dp", "seq")),
        P(("dp", "seq")),
        P(("dp", "seq")),
    )
    n_dp = mesh.shape["dp"]
    if mesh.shape["seq"] != 2 or n_dp & (n_dp - 1) != 0 or n_dp < 4:
        return jax.shard_map(
            body, mesh=mesh, in_specs=in_specs, out_specs=out_specs, check_vma=False
        )

    def chosen(*arrays):
        return fast_body(*arrays, n_dp=n_dp)

    return jax.shard_map(
        chosen, mesh=mesh, in_specs=in_specs, out_specs=out_specs, check_vma=False
    )
```

profile of v0, /device:TPU:0, one launch (start us, length us, event | category | flops | bytes accessed | tf_op | source)
XLA Modules:
  0.0 425.8 jit_solution(10632357173052434897)
XLA Ops:
  12.9 6.1 %concatenate.74 = bf16[288]{0:T(512)(128)(2,1)S(1)} concatenate(bf16[24]{0:T(256)(128)(2,1)} %param.21, bf16[24]{0:T(256)(128)(2,1)} %param.24, bf16[24]{0:T(256)(128)(2,1)} %param.26, bf16[24]{0:T(256)(128)(2,1)} %param.27, bf16[24]{0:T(256)(128)(2,1)} %param.28, bf16[24]{0:T(256)(128)(2,1)} %param.32, bf16[24]{0:T(256)(128)(2,1)} %param.33, bf16[24]{0:T(256)(128)(2,1)} %param.34, ...), dimensions={0} | concatenate | bytes 1152 | tf_op jit(solution)/shard_map/concatenate | solution.py:746
  28.3 11.2 %collective-permute-done.2 = bf16[2,32,1152]{2,1,0:T(8,128)(2,1)S(1)} collective-permute-done((bf16[2,32,1152]{2,1,0:T(8,128)(2,1)S(1)}, bf16[2,32,1152]{2,1,0:T(8,128)(2,1)S(1)}, u32[]{:S(2)}, u32[]{:S(2)}) %collective-permute-start.2) | collective-permute-done | bytes 147488 | tf_op jit(solution)/shard_map/ppermute | solution.py:650
  39.7 13.2 %collective-permute-done.3 = bf16[2,2,32,1152]{3,2,1,0:T(8,128)(2,1)S(1)} collective-permute-done((bf16[2,2,32,1152]{3,2,1,0:T(8,128)(2,1)S(1)}, bf16[2,2,32,1152]{3,2,1,0:T(8,128)(2,1)S(1)}, u32[]{:S(2)}, u32[]{:S(2)}) %collective-permute-start.3) | collective-permute-done | bytes 294944 | tf_op jit(solution)/shard_map/ppermute | solution.py:650
  55.9 13.2 %collective-permute-done.4 = bf16[2,2,2,32,1152]{4,3,2,1,0:T(8,128)(2,1)} collective-permute-done((bf16[2,2,2,32,1152]{4,3,2,1,0:T(8,128)(2,1)S(1)}, bf16[2,2,2,32,1152]{4,3,2,1,0:T(8,128)(2,1)}, u32[]{:S(2)}, u32[]{:S(2)}) %collective-permute-start.4) | collective-permute-done | bytes 589856 | tf_op jit(solution)/shard_map/ppermute | solution.py:650
  76.8 23.8 %collective-permute-done = bf16[1024,768]{1,0:T(8,128)(2,1)} collective-permute-done((bf16[1024,768]{1,0:T(8,128)(2,1)S(1)}, bf16[1024,768]{1,0:T(8,128)(2,1)}, u32[]{:S(2)}, u32[]{:S(2)}) %collective-permute-start) | collective-permute-done | bytes 1572896 | tf_op jit(solution)/shard_map/ppermute | solution.py:650
  106.4 8.9 %multiply_convert_fusion.1.qkv_ref = bf16[2048,1152]{1,0:T(8,128)(2,1)} fusion(bf16[768,1152]{1,0:T(8,128)(2,1)S(1)} %bitcast.242, f32[1152]{0:T(1024)S(1)} %copy-done.29, f32[1152]{0:T(1024)S(1)} %pad_maximum_fusion.20, bf16[1024,768]{1,0:T(8,128)(2,1)} %get-tuple-element.148, bf16[1024,768]{1,0:T(8,128)(2,1)} %get-tuple-element.147), kind=kOutput, calls=%fused_computation.9 | convolution fusion | flops 3637248000 | bytes 9643008 | tf_op jit(solution)/shard_map/dot_general | solution.py:52
  116.6 38.5 %attn_fwd.1 = (bf16[2048,384]{1,0:T(8,128)(2,1)}, f32[8,2048]{1,0:T(8,128)}) custom-call(s32[20]{0:T(128)} %bitcast.272, s32[16,1]{1,0:T(8,128)} %copy.153.posv_ref, s32[8,2048]{1,0:T(8,128)} %broadcast_in_dim.41.limit_ref, s32[8,2048]{1,0:T(8,128)} %broadcast_in_dim.42.write_ref, bf16[2048,1152]{1,0:T(8,128)(2,1)} %multiply_convert_fusion.1.qkv_ref), custom_call_target="tpu_custom_call" | custom-call | tf_op jit(solution)/shard_map/attn_fwd/pallas_call | solution.py:619
  164.3 5.4 %collective-permute-done.6 = bf16[1024,384]{1,0:T(8,128)(2,1)} collective-permute-done((bf16[1024,384]{1,0:T(8,128)(2,1)}, bf16[1024,384]{1,0:T(8,128)(2,1)}, u32[]{:S(2)}, u32[]{:S(2)}) %collective-permute-start.6) | collective-permute-done | bytes 786464 | tf_op jit(solution)/shard_map/ppermute | solution.py:650
  175.4 4.7 %slice.364 = bf16[32,96,768]{2,1,0:T(8,128)(2,1)S(1)} slice(bf16[32,216,768]{2,1,0:T(8,128)(2,1)} %bitcast.228), slice={[0:32], [120:216], [0:768]} | slice | bytes 9437184 | tf_op jit(solution)/shard_map/slice | solution.py:806
  183.2 14.9 %fusion.4 = (bf16[1024,3072]{1,0:T(8,128)(2,1)}, bf16[1024,3072]{1,0:T(8,128)(2,1)}) fusion(f32[3072]{0:T(1024)S(1)} %add.161, bf16[1024,768]{0,1:T(8,128)(2,1)S(1)} %fusion.14, bf16[768,768]{1,0:T(8,128)(2,1)S(1)} %bitcast.249, bf16[768,768]{1,0:T(8,128)(2,1)S(1)} %bitcast.251, bf16[768,768]{1,0:T(8,128)(2,1)S(1)} %bitcast.253, ...), kind=kOutput, calls=%fused_computation.5 | convolution fusion | flops 4888461312 | bytes 18886656 | tf_op jit(solution)/shard_map/dot_general | solution.py:52
  198.1 7.6 %fusion.103 = (f32[1024]{0:T(1024)S(1)}, f32[1024,768]{0,1:T(8,128)S(1)}) fusion(f32[768]{0:T(1024)S(1)} %add.168, bf16[1024,3072]{1,0:T(8,128)(2,1)} %get-tuple-element.28, bf16[3072,768]{1,0:T(8,128)(2,1)S(1)} %bitcast.239, f32[768]{0:T(1024)S(1)} %add.158, f32[768]{0:T(1024)S(1)} %mul.143, f32[1024]{0:T(1024)S(1)} %add_rsqrt_fusion.1, ...), kind=kOutput, calls=%fused_computation.222 | convolution fusion | flops 4837342208 | bytes 17323008 | tf_op jit(solution)/shard_map/dot_general | solution.py:52
  210.2 6.3 %convolution_convert_fusion = bf16[3072,768]{1,0:T(8,128)(2,1)S(1)} fusion(bf16[1024,3072]{1,0:T(8,128)(2,1)S(1)} %copy-done.31, bf16[1024,768]{0,1:T(8,128)(2,1)S(1)} %copy-done.3, f32[1024,768]{0,1:T(8,128)S(1)} %get-tuple-element.197, f32[1024]{0:T(1024)S(1)} %get-tuple-element.199, f32[1024]{0:T(1024)S(1)} %get-tuple-element.200, f32[768]{0:T(1024)S(1)} %mul.160, ...), kind=kOutput, calls=%fused_computation.12 | convolution fusion | flops 4841275392 | bytes 15748096 | tf_op jit(solution)/shard_map/ta,tb->ab/dot_general | solution.py:56
  216.5 10.2 %fusion.5 = (f32[3072]{0:T(1024)S(1)}, bf16[1024,3072]{1,0:T(8,128)(2,1)}) fusion(bf16[1024,3072]{1,0:T(8,128)(2,1)} %get-tuple-element.29, bf16[3072,768]{1,0:T(8,128)(2,1)S(1)} %bitcast.240, f32[1024]{0:T(1024)S(1)} %get-tuple-element.199, f32[1024,768]{0,1:T(8,128)S(1)} %get-tuple-element.197, f32[1024]{0:T(1024)S(1)} %broadcast_multiply_fusion.4, ...), kind=kOutput, calls=%fused_computation.10 | convolution fusion | flops 4851495936 | bytes 22051840 | tf_op jit(solution)/shard_map/tb,ab->ta/dot_general | solution.py:60
  241.3 11.2 %multiply_reduce_fusion = (f32[768]{0:T(1024)S(1)}, f32[1024]{0:T(1024)S(1)}, f32[1024]{0:T(1024)S(1)}, f32[768]{0:T(1024)S(1)}, f32[1024,768]{0,1:T(8,128)S(1)}) fusion(f32[1024,768]{0,1:T(8,128)S(1)} %get-tuple-element.195, f32[1024]{0:T(1024)S(1)} %add_rsqrt_fusion.1, f32[1024]{0:T(1024)S(1)} %broadcast_multiply_fusion.5, f32[768]{0:T(1024)S(1)} %mul.143, ...), kind=kOutput, calls=%fused_computation.29 | convolution fusion | flops 4864864256 | bytes 22065152 | tf_op jit(solution)/shard_map/tb,ab->ta/dot_general | solution.py:60
  264.9 3.8 collective-permute-done.7
  271.3 59.7 %attn_bwd.1 = (bf16[2048,1152]{1,0:T(8,128)(2,1)}, f32[8,384]{1,0:T(8,128)}) custom-call(s32[20]{0:T(128)} %bitcast.273, s32[16,1]{1,0:T(8,128)} %copy.153.posv_ref, s32[8,2048]{1,0:T(8,128)} %broadcast_in_dim.41.limit_ref, bf16[2048,1152]{1,0:T(8,128)(2,1)} %multiply_convert_fusion.1.qkv_ref, bf16[2048,384]{1,0:T(8,128)(2,1)} %pad_maximum_fusion.8.do_ref, ...), custom_call_target="tpu_custom_call" | custom-call | tf_op jit(solution)/shard_map/attn_bwd/pallas_call | solution.py:633
  332.4 6.5 %fusion.32 = bf16[1024,768]{0,1:T(8,128)(2,1)} fusion(bf16[768,1152]{1,0:T(8,128)(2,1)} %bitcast.243, pred[]{:T(512)S(6)} %eq.18, bf16[2048,1152]{1,0:T(8,128)(2,1)} %get-tuple-element.34), kind=kOutput, calls=%fused_computation.64 | convolution fusion | flops 1813905408 | bytes 8060929 | tf_op jit(solution)/shard_map/tb,ab->ta/dot_general | solution.py:60
  338.9 4.3 %fusion.28 = f32[768,1152]{1,0:T(8,128)S(1)} fusion(bf16[2048,1152]{1,0:T(8,128)(2,1)S(1)} %bitcast.275, bf16[1024,768]{1,0:T(8,128)(2,1)S(1)} %copy-done.16, bf16[1024,768]{1,0:T(8,128)(2,1)S(1)} %copy-done.15), kind=kOutput, calls=%fused_computation.60 | convolution fusion | flops 3630170112 | bytes 11403264 | tf_op jit(solution)/shard_map/ta,tb->ab/dot_general | solution.py:56
  345.9 4.8 %collective-permute-start.12 = (bf16[4,2,32,768]{3,2,1,0:T(8,128)(2,1)}, bf16[4,2,32,768]{3,2,1,0:T(8,128)(2,1)}, u32[]{:S(2)}, u32[]{:S(2)}) collective-permute-start(bf16[4,2,32,768]{3,2,1,0:T(8,128)(2,1)} %fusion.74), channel_id=1, source_target_pairs={{0,4},{2,6},{4,0},{6,2},{8,12},{10,14},{12,8},{14,10},{16,20},{18,... | collective-permute-start | bytes 1179656 | tf_op jit(solution)/shard_map/ppermute | solution.py:650
  356.3 4.7 %collective-permute-done.12 = bf16[4,2,32,768]{3,2,1,0:T(8,128)(2,1)} collective-permute-done((bf16[4,2,32,768]{3,2,1,0:T(8,128)(2,1)}, bf16[4,2,32,768]{3,2,1,0:T(8,128)(2,1)}, u32[]{:S(2)}, u32[]{:S(2)}) %collective-permute-start.12) | collective-permute-done | bytes 393248 | tf_op jit(solution)/shard_map/ppermute | solution.py:650
  362.6 12.8 %collective-permute-done.10 = bf16[4,2,32,1152]{3,2,1,0:T(8,128)(2,1)S(1)} collective-permute-done((bf16[4,2,32,1152]{3,2,1,0:T(8,128)(2,1)S(1)}, bf16[4,2,32,1152]{3,2,1,0:T(8,128)(2,1)S(1)}, u32[]{:S(2)}, u32[]{:S(2)}) %collective-permute-start.10) | collective-permute-done | bytes 589856 | tf_op jit(solution)/shard_map/ppermute | solution.py:650
  378.1 4.6 %fusion.29 = f32[1024,768]{0,1:T(8,128)S(1)} fusion(f32[1024,768]{0,1:T(8,128)S(1)} %copy-done.11, bf16[768,1152]{1,0:T(8,128)(2,1)S(1)} %bitcast.244, pred[]{:T(512)S(6)} %eq.18, bf16[2048,1152]{1,0:T(8,128)(2,1)} %get-tuple-element.34), kind=kOutput, calls=%fused_computation.63 | convolution fusion | flops 1813905408 | bytes 12779521 | tf_op jit(solution)/shard_map/tb,ab->ta/dot_general | solution.py:60
  382.7 6.9 %collective-permute-done.13 = bf16[2,2,32,1920]{3,2,1,0:T(8,128)(2,1)S(1)} collective-permute-done((bf16[2,2,32,1920]{3,2,1,0:T(8,128)(2,1)S(1)}, bf16[2,2,32,1920]{3,2,1,0:T(8,128)(2,1)S(1)}, u32[]{:S(2)}, u32[]{:S(2)}) %collective-permute-start.13) | collective-permute-done | bytes 491552 | tf_op jit(solution)/shard_map/ppermute | solution.py:650
  396.5 7.8 %collective-permute-done.14 = bf16[1,2,32,1920]{3,2,1,0:T(8,128)(2,1)S(1)} collective-permute-done((bf16[1,2,32,1920]{3,2,1,0:T(8,128)(2,1)}, bf16[1,2,32,1920]{3,2,1,0:T(8,128)(2,1)S(1)}, u32[]{:S(2)}, u32[]{:S(2)}) %collective-permute-start.14) | collective-permute-done | bytes 245792 | tf_op jit(solution)/shard_map/ppermute | solution.py:650
  (236 shorter events, 116.5 us)
Async XLA Ops:
  7.2 165.0 %all-gather.3.cloned.1.call-start = ((), (), s32[]{:S(2)}) async-start(), calls=%async_computation.2 | async-start | bytes 10948608 | tf_op jit(solution)/shard_map/all_gather | solution.py:744
  9.8 43.5 %copy-start.6 = (bf16[1024,768]{1,0:T(8,128)(2,1)S(1)}, bf16[1024,768]{1,0:T(8,128)(2,1)}, u32[]{:S(2)}) copy-start(bf16[1024,768]{1,0:T(8,128)(2,1)} %param.19) | copy-start | bytes 4718596
  9.9 405.4 %reduce-scatter.2.cloned.1.call-start = ((), (), s32[]{:S(2)}) async-start(), calls=%async_computation.1 | async-start | bytes 9732096 | tf_op jit(solution)/shard_map/reduce_scatter | solution.py:839
  19.1 6.3 %collective-permute-start.1 = (bf16[32,1152]{1,0:T(8,128)(2,1)S(1)}, bf16[32,1152]{1,0:T(8,128)(2,1)S(1)}, u32[]{:S(2)}, u32[]{:S(2)}) collective-permute-start(bf16[32,1152]{1,0:T(8,128)(2,1)S(1)} %fusion.79), channel_id=1, source_target_pairs={{0,1},{1,0},{2,3},{3,2},{4,5},{5,4},{6,7},{7,6},{8,9},{9,8},{10,11... | collective-permute-start | bytes 221192 | tf_op jit(solution)/shard_map/ppermute | solution.py:650
  25.4 14.1 %collective-permute-start.2 = (bf16[2,32,1152]{2,1,0:T(8,128)(2,1)S(1)}, bf16[2,32,1152]{2,1,0:T(8,128)(2,1)S(1)}, u32[]{:S(2)}, u32[]{:S(2)}) collective-permute-start(bf16[2,32,1152]{2,1,0:T(8,128)(2,1)S(1)} %pad_maximum_fusion.19), channel_id=1, source_target_pairs={{0,16},{2,18},{4,20},{6,22},{8,24},{10,26},{12,28},{14,30},{16,0},... | collective-permute-start | bytes 442376 | tf_op jit(solution)/shard_map/ppermute | solution.py:650
  39.6 13.3 %collective-permute-start.3 = (bf16[2,2,32,1152]{3,2,1,0:T(8,128)(2,1)S(1)}, bf16[2,2,32,1152]{3,2,1,0:T(8,128)(2,1)S(1)}, u32[]{:S(2)}, u32[]{:S(2)}) collective-permute-start(bf16[2,2,32,1152]{3,2,1,0:T(8,128)(2,1)S(1)} %pad_maximum_fusion.16), channel_id=1, source_target_pairs={{0,8},{2,10},{4,12},{6,14},{8,0},{10,2},{12,4},{14,6},{16,24},{18,... | collective-permute-start | bytes 884744 | tf_op jit(solution)/shard_map/ppermute | solution.py:650
  53.0 18.4 %copy-start.28 = (s32[1,2]{1,0:T(1,128)S(1)}, s32[1,2]{1,0:T(1,128)}, u32[]{:S(2)}) copy-start(s32[1,2]{1,0:T(1,128)} %param.36) | copy-start | bytes 28
  53.0 21.6 %copy-start.27 = (s32[1,20]{1,0:T(1,128)S(1)}, s32[1,20]{1,0:T(1,128)}, u32[]{:S(2)}) copy-start(s32[1,20]{1,0:T(1,128)} %param.37) | copy-start | bytes 244
  53.1 16.0 %collective-permute-start.4 = (bf16[2,2,2,32,1152]{4,3,2,1,0:T(8,128)(2,1)S(1)}, bf16[2,2,2,32,1152]{4,3,2,1,0:T(8,128)(2,1)}, u32[]{:S(2)}, u32[]{:S(2)}) collective-permute-start(bf16[2,2,2,32,1152]{4,3,2,1,0:T(8,128)(2,1)S(1)} %pad_maximum_fusion.14), channel_id=1, source_target_pairs={{0,4},{2,6},{4,0},{6,2},{8,12},{10,14},{12,8},{14,10},{16,20},{18,... | collective-permute-start | bytes 1769480 | tf_op jit(solution)/shard_map/ppermute | solution.py:650
  53.3 47.3 %collective-permute-start = (bf16[1024,768]{1,0:T(8,128)(2,1)S(1)}, bf16[1024,768]{1,0:T(8,128)(2,1)}, u32[]{:S(2)}, u32[]{:S(2)}) collective-permute-start(bf16[1024,768]{1,0:T(8,128)(2,1)S(1)} %copy-done.6), channel_id=1, source_target_pairs={{0,1},{1,0},{2,3},{3,2},{4,5},{5,4},{6,7},{7,6},{8,9},{9,8},{10,11... | collective-permute-start | bytes 4718600 | tf_op jit(solution)/shard_map/ppermute | solution.py:650
  71.4 32.5 %collective-permute-start.5 = (bf16[2,2,2,2,32,1152]{5,4,3,2,1,0:T(8,128)(2,1)}, bf16[2,2,2,2,32,1152]{5,4,3,2,1,0:T(8,128)(2,1)}, u32[]{:S(2)}, u32[]{:S(2)}) collective-permute-start(bf16[2,2,2,2,32,1152]{5,4,3,2,1,0:T(8,128)(2,1)} %pad_maximum_fusion.9), channel_id=1, source_target_pairs={{0,2},{2,0},{4,6},{6,4},{8,10},{10,8},{12,14},{14,12},{16,18},{18,... | collective-permute-start | bytes 3538952 | tf_op jit(solution)/shard_map/ppermute | solution.py:650
  106.1 9.2 %copy-start.12 = (bf16[32,24,1152]{2,1,0:T(8,128)(2,1)}, bf16[32,24,1152]{2,1,0:T(8,128)(2,1)S(1)}, u32[]{:S(2)}) copy-start(bf16[32,24,1152]{2,1,0:T(8,128)(2,1)S(1)} %slice.349) | copy-start | bytes 5308420
  157.4 12.3 %copy-start.2 = (bf16[2048,384]{1,0:T(8,128)(2,1)S(1)}, bf16[2048,384]{1,0:T(8,128)(2,1)}, u32[]{:S(2)}) copy-start(bf16[2048,384]{1,0:T(8,128)(2,1)} %get-tuple-element.27.o_ref) | copy-start | bytes 4718596
  157.4 12.3 %collective-permute-start.6 = (bf16[1024,384]{1,0:T(8,128)(2,1)}, bf16[1024,384]{1,0:T(8,128)(2,1)}, u32[]{:S(2)}, u32[]{:S(2)}) collective-permute-start(bf16[1024,384]{1,0:T(8,128)(2,1)} %broadcast_select_fusion.9), channel_id=1, source_target_pairs={{0,1},{1,0},{2,3},{3,2},{4,5},{5,4},{6,7},{7,6},{8,9},{9,8},{10,11... | collective-permute-start | bytes 2359304 | tf_op jit(solution)/shard_map/ppermute | solution.py:650
  205.7 10.7 %copy-start = (f32[1024,768]{0,1:T(8,128)}, f32[1024,768]{0,1:T(8,128)S(1)}, u32[]{:S(2)}) copy-start(f32[1024,768]{0,1:T(8,128)S(1)} %get-tuple-element.197) | copy-start | bytes 9437188
  256.4 12.3 %collective-permute-start.7 = (bf16[1024,384]{1,0:T(8,128)(2,1)}, bf16[1024,384]{1,0:T(8,128)(2,1)}, u32[]{:S(2)}, u32[]{:S(2)}) collective-permute-start(bf16[1024,384]{1,0:T(8,128)(2,1)} %broadcast_select_fusion.5), channel_id=1, source_target_pairs={{0,1},{1,0},{2,3},{3,2},{4,5},{5,4},{6,7},{7,6},{8,9},{9,8},{10,11... | collective-permute-start | bytes 2359304 | tf_op jit(solution)/shard_map/ppermute | solution.py:650
  264.9 78.6 %collective-permute-start.11 = (bf16[8,2,32,768]{3,2,1,0:T(8,128)(2,1)}, bf16[8,2,32,768]{3,2,1,0:T(8,128)(2,1)}, u32[]{:S(2)}, u32[]{:S(2)}) collective-permute-start(bf16[8,2,32,768]{3,2,1,0:T(8,128)(2,1)} %fusion.66), channel_id=1, source_target_pairs={{0,2},{2,0},{4,6},{6,4},{8,10},{10,8},{12,14},{14,12},{16,18},{18,... | collective-permute-start | bytes 2359304 | tf_op jit(solution)/shard_map/ppermute | solution.py:650
  343.4 7.3 %collective-permute-start.9 = (bf16[8,2,32,1152]{3,2,1,0:T(8,128)(2,1)S(1)}, bf16[8,2,32,1152]{3,2,1,0:T(8,128)(2,1)S(1)}, u32[]{:S(2)}, u32[]{:S(2)}) collective-permute-start(bf16[8,2,32,1152]{3,2,1,0:T(8,128)(2,1)S(1)} %fusion.58), channel_id=1, source_target_pairs={{0,2},{2,0},{4,6},{6,4},{8,10},{10,8},{12,14},{14,12},{16,18},{18,... | collective-permute-start | bytes 3538952 | tf_op jit(solution)/shard_map/ppermute | solution.py:650
  345.9 15.1 %collective-permute-start.12 = (bf16[4,2,32,768]{3,2,1,0:T(8,128)(2,1)}, bf16[4,2,32,768]{3,2,1,0:T(8,128)(2,1)}, u32[]{:S(2)}, u32[]{:S(2)}) collective-permute-start(bf16[4,2,32,768]{3,2,1,0:T(8,128)(2,1)} %fusion.74), channel_id=1, source_target_pairs={{0,4},{2,6},{4,0},{6,2},{8,12},{10,14},{12,8},{14,10},{16,20},{18,... | collective-permute-start | bytes 1179656 | tf_op jit(solution)/shard_map/ppermute | solution.py:650
  351.2 24.3 %collective-permute-start.10 = (bf16[4,2,32,1152]{3,2,1,0:T(8,128)(2,1)S(1)}, bf16[4,2,32,1152]{3,2,1,0:T(8,128)(2,1)S(1)}, u32[]{:S(2)}, u32[]{:S(2)}) collective-permute-start(bf16[4,2,32,1152]{3,2,1,0:T(8,128)(2,1)S(1)} %fusion.72), channel_id=1, source_target_pairs={{0,4},{2,6},{4,0},{6,2},{8,12},{10,14},{12,8},{14,10},{16,20},{18,... | collective-permute-start | bytes 1769480 | tf_op jit(solution)/shard_map/ppermute | solution.py:650
  354.6 38.8 %collective-permute-start.8 = (bf16[1024,768]{0,1:T(8,128)(2,1)}, bf16[1024,768]{0,1:T(8,128)(2,1)S(1)}, u32[]{:S(2)}, u32[]{:S(2)}) collective-permute-start(bf16[1024,768]{0,1:T(8,128)(2,1)} %fusion.32), channel_id=1, source_target_pairs={{0,1},{1,0},{2,3},{3,2},{4,5},{5,4},{6,7},{7,6},{8,9},{9,8},{10,11... | collective-permute-start | bytes 4718600 | tf_op jit(solution)/shard_map/ppermute | solution.py:650
  375.9 13.7 %collective-permute-start.13 = (bf16[2,2,32,1920]{3,2,1,0:T(8,128)(2,1)S(1)}, bf16[2,2,32,1920]{3,2,1,0:T(8,128)(2,1)S(1)}, u32[]{:S(2)}, u32[]{:S(2)}) collective-permute-start(bf16[2,2,32,1920]{3,2,1,0:T(8,128)(2,1)S(1)} %fusion.73), channel_id=1, source_target_pairs={{0,8},{2,10},{4,12},{6,14},{8,0},{10,2},{12,4},{14,6},{16,24},{18,... | collective-permute-start | bytes 1474568 | tf_op jit(solution)/shard_map/ppermute | solution.py:650
  390.6 13.7 %collective-permute-start.14 = (bf16[1,2,32,1920]{3,2,1,0:T(8,128)(2,1)}, bf16[1,2,32,1920]{3,2,1,0:T(8,128)(2,1)S(1)}, u32[]{:S(2)}, u32[]{:S(2)}) collective-permute-start(bf16[1,2,32,1920]{3,2,1,0:T(8,128)(2,1)} %fusion.75), channel_id=1, source_target_pairs={{0,16},{2,18},{4,20},{6,22},{8,24},{10,26},{12,28},{14,30},{16,0},... | collective-permute-start | bytes 737288 | tf_op jit(solution)/shard_map/ppermute | solution.py:650
  405.5 5.0 %collective-permute-start.15 = (bf16[32,1920]{1,0:T(8,128)(2,1)S(1)}, bf16[32,1920]{1,0:T(8,128)(2,1)S(1)}, u32[]{:S(2)}, u32[]{:S(2)}) collective-permute-start(bf16[32,1920]{1,0:T(8,128)(2,1)S(1)} %fusion.78), channel_id=1, source_target_pairs={{0,1},{1,0},{2,3},{3,2},{4,5},{5,4},{6,7},{7,6},{8,9},{9,8},{10,11... | collective-permute-start | bytes 368648 | tf_op jit(solution)/shard_map/ppermute | solution.py:650
  (28 other events, 141.9 us)
Sparse Core Ops, SparseCore 0:
  10.9 108.3 all-gather.2
  241.4 139.6 reduce-scatter.1
where the time goes:
time: 430 us; the launch traced here: 426 us
  waiting for transfers between devices  110 us (26%)
  Pallas kernels  98.1 us (23%)
  matrix products  86.3 us (20%)
  local copies, waits for them, and re-layouts  52.6 us (12%)
  other arithmetic  36.8 us (9%)
  starting transfers between devices  23.9 us (6%)
  between operations  18.2 us (4%)
    ppermute x16, waiting for transfers between devices, bit_swap(): return lax.ppermute(x, axis, [(i, i ^ bit) for i in range(size)])  110 us
    pallas_call x1, Pallas kernels, attn_bwd(): pl.pallas_call(partial(bwd_kernel, bq=bq, scale=scale, np_=np_), grid=(1,...  59.7 us
    pallas_call x1, Pallas kernels, attn_fwd(): pl.pallas_call(partial(fwd_kernel, bq=bq, np_=np_, qb0=qb0, qb1=L // bq i...  38.5 us
    dot_general x5, matrix products, back_product(): jnp.einsum('tb,ab->ta', gradient, weight, preferred_element_type=jnp.floa...  34 us
    dot_general x4, matrix products, dense(): return jnp.dot(left, right, preferred_element_type=jnp.float32)  33 us
    ppermute x16, starting transfers between devices, bit_swap(): return lax.ppermute(x, axis, [(i, i ^ bit) for i in range(size)])  23.9 us
    unnamed x83, local copies, waits for them, and re-layouts  22.4 us
    dot_general x7, matrix products, outer_product(): jnp.einsum('ta,tb->ab', left, right, preferred_element_type=jnp.float32)  19.2 us
  transfers between devices with their start and end apart: 18, of which 13 were waited for; matrix products, arithmetic and copies ran while one was open for 23% of the time, Pallas kernels for 23%

commit v1 on v0

--- a/solution.py
+++ b/solution.py
@@ -640,6 +640,7 @@
     )(pos,posv,limit,qkv,do,o,lse)
 
 
+LANES = 128
 LOG2E = 1.4426950408889634
 ALL = ("dp", "seq")
 RSQRT2 = 0.7071067811865476
@@ -685,6 +686,11 @@
     keep = jnp.where(up, rest[:, 1], rest[:, 0])
     got = bit_swap(give, "dp", size, bit)
     return keep + got.astype(F32)
+
+
+def spread_lanes(rows, part):
+    rows = jnp.pad(rows, ((0, 0), (0, part * LANES - rows.shape[1])))
+    return rows.reshape(rows.shape[0], part, LANES)
 
 
 def norm_parts(values):
@@ -759,20 +765,19 @@
     count = vectors.shape[0]
     three = jnp.stack([query_weight, key_weight, value_weight], 1)
     three = three.reshape(part, 3, 2, half)
-    line = jnp.pad(vectors, (0, 3 * half - count))[None, :]
-    line = jnp.pad(line, ((0, 7), (0, 0)))
+    line = jnp.pad(vectors, (0, part * LANES - count)).reshape(part, LANES)
 
     def columns(upper_half):
         kept = jnp.where(upper_half, three[:, :, 1], three[:, :, 0]).reshape(part, 3 * half)
-        return jnp.concatenate([kept, line], 0)
+        return jnp.concatenate([kept, line], 1)
 
     pair = side(upper, columns(upper)[None], swap(columns(jnp.logical_not(upper)))[None], 0)
-    early = gather_dp(pair, n_dp).reshape(devices, part + 8, 3 * half)
-    w_three = early[:, :part].reshape(width, 3 * half)
-    lines = early[:, part, :count].astype(F32)
+    early = gather_dp(pair, n_dp).reshape(width, 3 * half + LANES)
+    w_three = early[:, : 3 * half]
+    lines = early[:, 3 * half :].astype(F32).reshape(devices, part * LANES)
     vector = lambda k: lines[:, k * part : (k + 1) * part].reshape(width)
     b_query, b_value, b_output, g_first, s_first, b_outer, g_second, s_second = map(vector, range(8))
-    b_inner = lines[:, 8 * part :].reshape(inner_width)
+    b_inner = lines[:, 8 * part : count].reshape(inner_width)
     own_half = lambda v: jnp.where(upper, v[half:], v[:half])
     features = side(upper, inputs, peer_inputs, 0)
     scale = HD ** (-0.5)
@@ -861,10 +866,11 @@
     thin = jnp.concatenate(
         [v.reshape(devices, part) for v in thin] + [grad_inner_bias.reshape(devices, inner_part)], 1
     )
-    thin = jnp.pad(thin[:, None, :], ((0, 0), (0, 7), (0, width - thin.shape[1])))
-    mid = jnp.concatenate([grad_output_weight, thin], 1).reshape(n_dp, 2, part + 8, width)
+    mid = jnp.concatenate([grad_output_weight, spread_lanes(thin, part)], 2)
+    mid = mid.reshape(n_dp, 2, part, width + LANES)
     bits = bits_of(n_dp)
     mid = halve_dp(mid, n_dp, bits[0])
+    mid = halve_dp(mid, n_dp, bits[1])
     grads, bias_sums = attn_bwd(
         qkv, memories, reads, limit, grad_heads, out_heads, totals, pairs, scale
     )
@@ -876,11 +882,11 @@
     three_grad = outer_product(features, grads).reshape(devices, part, 3 * half)
     full = lambda v: side(upper, v, jnp.zeros_like(v), 0).reshape(devices, part)
     tails = jnp.concatenate([full(bias_sums[0]), full(bias_sums[1])], 1)
-    tails = jnp.pad(tails[:, None, :], ((0, 0), (0, 7), (0, 3 * half - 2 * part)))
-    blocks = jnp.concatenate([three_grad, tails], 1).reshape(n_dp, 2, part + 8, 3 * half)
+    blocks = jnp.concatenate([three_grad, spread_lanes(tails, part)], 2)
+    wide_half = 3 * half + LANES
+    blocks = blocks.reshape(n_dp, 2, part, wide_half)
     blocks = halve_dp(blocks, n_dp, bits[0])
     own_part = lax.optimization_barrier(grad_mixed + back_product(own_grads, w_three))
-    mid = halve_dp(mid, n_dp, bits[1])
     blocks = halve_dp(blocks, n_dp, bits[1])
     blocks = jnp.concatenate([blocks, mid], 3)
     for bit in bits[2:]:
@@ -890,12 +896,15 @@
     keep = jnp.where(upper, mine[1], mine[0])
     got = swap(give.astype(BF)).astype(F32)
     grad_inputs = own_part + sent.astype(F32)
-    total = keep[:, 3 * half :] + got[:, 3 * half :]
-    tail_sum = keep[part, : 2 * part] + got[part, : 2 * part]
-    keep = keep[:part, : 3 * half].reshape(part, 3, half)
-    got = got[:part, : 3 * half].reshape(part, 3, half)
+    total = keep[:, wide_half : wide_half + width] + got[:, wide_half : wide_half + width]
+    ends = lambda x: x[:, wide_half + width :].reshape(-1)
+    thin_sum = ends(keep) + ends(got)
+    ends = lambda x: x[:, 3 * half : wide_half].reshape(-1)
+    tail_sum = ends(keep) + ends(got)
+    keep = keep[:, : 3 * half].reshape(part, 3, half)
+    got = got[:, : 3 * half].reshape(part, 3, half)
     matrices = side(upper, keep, got, 2)
-    thin_part = lambda k: total[part, k * part : (k + 1) * part]
+    thin_part = lambda k: thin_sum[k * part : (k + 1) * part]
     reduced = reduced.astype(F32)
     own_inner = jnp.concatenate([reduced[k * part : (k + 1) * part] for k in range(ratio)], 1)
     own_outer = reduced[ratio * part :]
@@ -906,13 +915,13 @@
         tail_sum[:part],
         matrices[:, 1],
         matrices[:, 2],
-        tail_sum[part:],
-        total[:part],
+        tail_sum[part : 2 * part],
+        total,
         thin_part(0),
         thin_part(1),
         thin_part(2),
         own_inner,
-        total[part, 6 * part : 6 * part + inner_part],
+        thin_sum[6 * part : 6 * part + inner_part],
         own_outer,
         thin_part(3),
         thin_part(4),

time: 430 us -> 430 us (level)
  waiting for transfers between devices: 110 us -> 104 us
    ppermute x16, waiting for transfers between devices: 110 us -> 104 us  [bit_swap(): return lax.ppermute(x, axis, [(i, i ^ bit) for i in range(size)])]
    ppermute x16, starting transfers between devices: 23.9 us -> 19.5 us  [bit_swap(): return lax.ppermute(x, axis, [(i, i ^ bit) for i in range(size)])]
    unnamed x83 -> x97, local copies, waits for them, and re-layouts: 22.4 us -> 23.9 us
  transfers between devices with their start and end apart: 18 -> 18, of which waited for: 13 -> 13; matrix products, arithmetic and copies ran while one was open for 23% -> 25% of each run, Pallas kernels for 23% -> 23%
where the time goes in v1:
time: 430 us; the launch traced here: 423 us
  waiting for transfers between devices  104 us (24%)
  Pallas kernels  98.2 us (23%)
  matrix products  90.4 us (21%)
  local copies, waits for them, and re-layouts  53.8 us (13%)
  other arithmetic  38.8 us (9%)
  starting transfers between devices  19.6 us (5%)
  between operations  18.2 us (4%)
    ppermute x16, waiting for transfers between devices, bit_swap(): return lax.ppermute(x, axis, [(i, i ^ bit) for i in range(size)])  104 us
    pallas_call x1, Pallas kernels, attn_bwd(): pl.pallas_call(partial(bwd_kernel, bq=bq, scale=scale, np_=np_), grid=(1,...  59.7 us
    pallas_call x1, Pallas kernels, attn_fwd(): pl.pallas_call(partial(fwd_kernel, bq=bq, np_=np_, qb0=qb0, qb1=L // bq i...  38.5 us
    dot_general x5, matrix products, back_product(): jnp.einsum('tb,ab->ta', gradient, weight, preferred_element_type=jnp.floa...  35.7 us
    dot_general x4, matrix products, dense(): return jnp.dot(left, right, preferred_element_type=jnp.float32)  32.9 us
    unnamed x97, local copies, waits for them, and re-layouts  23.9 us
    dot_general x7, matrix products, outer_product(): jnp.einsum('ta,tb->ab', left, right, preferred_element_type=jnp.float32)  21.8 us
    ppermute x16, starting transfers between devices, bit_swap(): return lax.ppermute(x, axis, [(i, i ^ bit) for i in range(size)])  19.5 us
  transfers between devices with their start and end apart: 18, of which 13 were waited for; matrix products, arithmetic and copies ran while one was open for 25% of the time, Pallas kernels for 23%

profile of v1, /device:TPU:0, one launch (start us, length us, event | category | flops | bytes accessed | tf_op | source)
XLA Modules:
  0.0 422.8 jit_solution(14687766301806172415)
XLA Ops:
  12.9 6.1 %concatenate.74 = bf16[288]{0:T(512)(128)(2,1)S(1)} concatenate(bf16[24]{0:T(256)(128)(2,1)} %param.21, bf16[24]{0:T(256)(128)(2,1)} %param.24, bf16[24]{0:T(256)(128)(2,1)} %param.26, bf16[24]{0:T(256)(128)(2,1)} %param.27, bf16[24]{0:T(256)(128)(2,1)} %param.28, bf16[24]{0:T(256)(128)(2,1)} %param.32, bf16[24]{0:T(256)(128)(2,1)} %param.33, bf16[24]{0:T(256)(128)(2,1)} %param.34, ...), dimensions={0} | concatenate | bytes 1152 | tf_op jit(solution)/shard_map/concatenate | solution.py:752
  27.9 10.6 %collective-permute-done.2 = bf16[2,24,1280]{2,1,0:T(8,128)(2,1)S(1)} collective-permute-done((bf16[2,24,1280]{2,1,0:T(8,128)(2,1)S(1)}, bf16[2,24,1280]{2,1,0:T(8,128)(2,1)S(1)}, u32[]{:S(2)}, u32[]{:S(2)}) %collective-permute-start.2) | collective-permute-done | bytes 122912 | tf_op jit(solution)/shard_map/ppermute | solution.py:651
  38.6 6.8 %collective-permute-done.3 = bf16[2,2,24,1280]{3,2,1,0:T(8,128)(2,1)S(1)} collective-permute-done((bf16[2,2,24,1280]{3,2,1,0:T(8,128)(2,1)S(1)}, bf16[2,2,24,1280]{3,2,1,0:T(8,128)(2,1)S(1)}, u32[]{:S(2)}, u32[]{:S(2)}) %collective-permute-start.3) | collective-permute-done | bytes 245792 | tf_op jit(solution)/shard_map/ppermute | solution.py:651
  48.6 17.8 %collective-permute-done.4 = bf16[2,2,2,24,1280]{4,3,2,1,0:T(8,128)(2,1)} collective-permute-done((bf16[2,2,2,24,1280]{4,3,2,1,0:T(8,128)(2,1)S(1)}, bf16[2,2,2,24,1280]{4,3,2,1,0:T(8,128)(2,1)}, u32[]{:S(2)}, u32[]{:S(2)}) %collective-permute-start.4) | collective-permute-done | bytes 491552 | tf_op jit(solution)/shard_map/ppermute | solution.py:651
  73.9 17.9 %collective-permute-done = bf16[1024,768]{1,0:T(8,128)(2,1)} collective-permute-done((bf16[1024,768]{1,0:T(8,128)(2,1)S(1)}, bf16[1024,768]{1,0:T(8,128)(2,1)}, u32[]{:S(2)}, u32[]{:S(2)}) %collective-permute-start) | collective-permute-done | bytes 1572896 | tf_op jit(solution)/shard_map/ppermute | solution.py:651
  98.4 8.9 %multiply_convert_fusion.1.qkv_ref = bf16[2048,1152]{1,0:T(8,128)(2,1)} fusion(f32[1152]{0:T(1024)S(1)} %copy-done.35, f32[1152]{0:T(1024)S(1)} %pad_maximum_fusion.22, bf16[1024,768]{1,0:T(8,128)(2,1)} %get-tuple-element.148, bf16[1024,768]{1,0:T(8,128)(2,1)} %get-tuple-element.147, bf16[768,1280]{1,0:T(8,128)(2,1)} %bitcast.227), kind=kOutput, calls=%fused_computation.9 | convolution fusion | flops 3637248000 | bytes 9643008 | tf_op jit(solution)/shard_map/dot_general | solution.py:52
  108.6 38.5 %attn_fwd.1 = (bf16[2048,384]{1,0:T(8,128)(2,1)}, f32[8,2048]{1,0:T(8,128)}) custom-call(s32[20]{0:T(128)} %bitcast.253, s32[16,1]{1,0:T(8,128)} %copy.151.posv_ref, s32[8,2048]{1,0:T(8,128)} %broadcast_in_dim.16.limit_ref, s32[8,2048]{1,0:T(8,128)} %broadcast_in_dim.17.write_ref, bf16[2048,1152]{1,0:T(8,128)(2,1)} %multiply_convert_fusion.1.qkv_ref), custom_call_target="tpu_custom_call" | custom-call | tf_op jit(solution)/shard_map/attn_fwd/pallas_call | solution.py:619
  155.3 12.1 %collective-permute-done.6 = bf16[1024,384]{1,0:T(8,128)(2,1)} collective-permute-done((bf16[1024,384]{1,0:T(8,128)(2,1)}, bf16[1024,384]{1,0:T(8,128)(2,1)}, u32[]{:S(2)}, u32[]{:S(2)}) %collective-permute-start.6) | collective-permute-done | bytes 786464 | tf_op jit(solution)/shard_map/ppermute | solution.py:651
  173.1 4.7 %slice.360 = bf16[32,96,768]{2,1,0:T(8,128)(2,1)S(1)} slice(bf16[32,216,768]{2,1,0:T(8,128)(2,1)} %bitcast.212), slice={[0:32], [120:216], [0:768]} | slice | bytes 9437184 | tf_op jit(solution)/shard_map/slice | solution.py:811
  181.0 14.4 %fusion.4 = (bf16[1024,3072]{1,0:T(8,128)(2,1)}, bf16[1024,3072]{1,0:T(8,128)(2,1)}) fusion(f32[3072]{0:T(1024)S(1)} %add.167, bf16[1024,768]{0,1:T(8,128)(2,1)S(1)} %fusion.14, bf16[768,768]{1,0:T(8,128)(2,1)S(1)} %bitcast.234, bf16[768,768]{1,0:T(8,128)(2,1)S(1)} %bitcast.236, bf16[768,768]{1,0:T(8,128)(2,1)S(1)} %bitcast.238, ...), kind=kOutput, calls=%fused_computation.5 | convolution fusion | flops 4888461312 | bytes 18886656 | tf_op jit(solution)/shard_map/dot_general | solution.py:52
  195.4 8.0 %fusion.109 = (f32[1024]{0:T(1024)S(1)}, f32[1024,768]{0,1:T(8,128)S(1)}) fusion(f32[768]{0:T(1024)S(1)} %add.174, bf16[1024,3072]{1,0:T(8,128)(2,1)} %get-tuple-element.28, bf16[3072,768]{1,0:T(8,128)(2,1)S(1)} %bitcast.219, f32[768]{0:T(1024)S(1)} %add.164, f32[768]{0:T(1024)S(1)} %mul.143, f32[1024]{0:T(1024)S(1)} %add_rsqrt_fusion.1, ...), kind=kOutput, calls=%fused_computation.224 | convolution fusion | flops 4837342208 | bytes 17323008 | tf_op jit(solution)/shard_map/dot_general | solution.py:52
  207.8 6.3 %convolution_convert_fusion = bf16[3072,768]{1,0:T(8,128)(2,1)S(1)} fusion(bf16[1024,3072]{1,0:T(8,128)(2,1)S(1)} %copy-done.37, bf16[1024,768]{0,1:T(8,128)(2,1)S(1)} %copy-done.3, f32[1024,768]{0,1:T(8,128)S(1)} %get-tuple-element.199, f32[1024]{0:T(1024)S(1)} %get-tuple-element.201, f32[1024]{0:T(1024)S(1)} %get-tuple-element.202, f32[768]{0:T(1024)S(1)} %mul.160, ...), kind=kOutput, calls=%fused_computation.12 | convolution fusion | flops 4841275392 | bytes 15748096 | tf_op jit(solution)/shard_map/ta,tb->ab/dot_general | solution.py:56
  214.2 10.8 %fusion.5 = (f32[3072]{0:T(1024)}, bf16[1024,3072]{1,0:T(8,128)(2,1)}) fusion(bf16[1024,3072]{1,0:T(8,128)(2,1)} %get-tuple-element.29, bf16[3072,768]{1,0:T(8,128)(2,1)S(1)} %bitcast.220, f32[1024]{0:T(1024)S(1)} %get-tuple-element.201, f32[1024,768]{0,1:T(8,128)S(1)} %get-tuple-element.199, f32[1024]{0:T(1024)S(1)} %broadcast_multiply_fusion.4, ...), kind=kOutput, calls=%fused_computation.10 | convolution fusion | flops 4851495936 | bytes 22051840 | tf_op jit(solution)/shard_map/tb,ab->ta/dot_general | solution.py:60
  239.6 11.8 %multiply_reduce_fusion = (f32[768]{0:T(1024)}, f32[1024]{0:T(1024)S(1)}, f32[1024]{0:T(1024)S(1)}, f32[768]{0:T(1024)}, f32[1024,768]{0,1:T(8,128)S(1)}) fusion(f32[1024,768]{0,1:T(8,128)S(1)} %get-tuple-element.197, f32[1024]{0:T(1024)S(1)} %add_rsqrt_fusion.1, f32[1024]{0:T(1024)S(1)} %broadcast_multiply_fusion.5, f32[768]{0:T(1024)S(1)} %mul.143, ...), kind=kOutput, calls=%fused_computation.27 | convolution fusion | flops 4864864256 | bytes 22065152 | tf_op jit(solution)/shard_map/tb,ab->ta/dot_general | solution.py:60
  260.9 4.0 fusion.61
  265.9 5.4 %collective-permute-done.7 = bf16[1024,384]{1,0:T(8,128)(2,1)} collective-permute-done((bf16[1024,384]{1,0:T(8,128)(2,1)S(1)}, bf16[1024,384]{1,0:T(8,128)(2,1)}, u32[]{:S(2)}, u32[]{:S(2)}) %collective-permute-start.7) | collective-permute-done | bytes 786464 | tf_op jit(solution)/shard_map/ppermute | solution.py:651
  274.1 59.7 %attn_bwd.1 = (bf16[2048,1152]{1,0:T(8,128)(2,1)}, f32[8,384]{1,0:T(8,128)}) custom-call(s32[20]{0:T(128)} %bitcast.254, s32[16,1]{1,0:T(8,128)} %copy.151.posv_ref, s32[8,2048]{1,0:T(8,128)} %broadcast_in_dim.16.limit_ref, bf16[2048,1152]{1,0:T(8,128)(2,1)} %multiply_convert_fusion.1.qkv_ref, bf16[2048,384]{1,0:T(8,128)(2,1)} %pad_maximum_fusion.7.do_ref, ...), custom_call_target="tpu_custom_call" | custom-call | tf_op jit(solution)/shard_map/attn_bwd/pallas_call | solution.py:633
  335.1 7.0 %fusion.32 = bf16[1024,768]{0,1:T(8,128)(2,1)} fusion(pred[]{:T(512)S(6)} %eq.18, bf16[2048,1152]{1,0:T(8,128)(2,1)} %get-tuple-element.34, bf16[768,1280]{1,0:T(8,128)(2,1)} %bitcast.228), kind=kOutput, calls=%fused_computation.63 | convolution fusion | flops 1813905408 | bytes 8060929 | tf_op jit(solution)/shard_map/tb,ab->ta/dot_general | solution.py:60
  342.1 4.3 %fusion.25 = f32[768,1152]{1,0:T(8,128)S(1)} fusion(bf16[2048,1152]{1,0:T(8,128)(2,1)S(1)} %bitcast.256, bf16[1024,768]{1,0:T(8,128)(2,1)S(1)} %copy-done.16, bf16[1024,768]{1,0:T(8,128)(2,1)S(1)} %copy-done.15), kind=kOutput, calls=%fused_computation.53 | convolution fusion | flops 3630170112 | bytes 11403264 | tf_op jit(solution)/shard_map/ta,tb->ab/dot_general | solution.py:56
  356.5 4.0 collective-permute-done.12
  361.6 11.4 %collective-permute-done.10 = bf16[4,2,24,1280]{3,2,1,0:T(8,128)(2,1)} collective-permute-done((bf16[4,2,24,1280]{3,2,1,0:T(8,128)(2,1)}, bf16[4,2,24,1280]{3,2,1,0:T(8,128)(2,1)}, u32[]{:S(2)}, u32[]{:S(2)}) %collective-permute-start.10) | collective-permute-done | bytes 491552 | tf_op jit(solution)/shard_map/ppermute | solution.py:651
  376.2 4.6 %fusion.29 = f32[1024,768]{0,1:T(8,128)S(1)} fusion(f32[1024,768]{0,1:T(8,128)S(1)} %copy-done.11, pred[]{:T(512)S(6)} %eq.18, bf16[2048,1152]{1,0:T(8,128)(2,1)} %get-tuple-element.34, bf16[768,1280]{1,0:T(8,128)(2,1)S(1)} %bitcast.229), kind=kOutput, calls=%fused_computation.62 | convolution fusion | flops 1813905408 | bytes 12779521 | tf_op jit(solution)/shard_map/tb,ab->ta/dot_general | solution.py:60
  380.9 5.1 %collective-permute-done.13 = bf16[2,2,24,2176]{3,2,1,0:T(8,128)(2,1)S(1)} collective-permute-done((bf16[2,2,24,2176]{3,2,1,0:T(8,128)(2,1)S(1)}, bf16[2,2,24,2176]{3,2,1,0:T(8,128)(2,1)S(1)}, u32[]{:S(2)}, u32[]{:S(2)}) %collective-permute-start.13) | collective-permute-done | bytes 417824 | tf_op jit(solution)/shard_map/ppermute | solution.py:651
  397.4 4.2 collective-permute-done.14
  (245 shorter events, 120.2 us)
Async XLA Ops:
  7.2 162.7 %all-gather.3.cloned.1.call-start = ((), (), s32[]{:S(2)}) async-start(), calls=%async_computation.2 | async-start | bytes 10948608 | tf_op jit(solution)/shard_map/all_gather | solution.py:750
  7.2 39.8 %copy-start.7 = (bf16[1024,768]{1,0:T(8,128)(2,1)S(1)}, bf16[1024,768]{1,0:T(8,128)(2,1)}, u32[]{:S(2)}) copy-start(bf16[1024,768]{1,0:T(8,128)(2,1)} %param.19) | copy-start | bytes 4718596
  10.0 402.3 %reduce-scatter.2.cloned.1.call-start = ((), (), s32[]{:S(2)}) async-start(), calls=%async_computation.1 | async-start | bytes 9732096 | tf_op jit(solution)/shard_map/reduce_scatter | solution.py:844
  19.1 5.9 %collective-permute-start.1 = (bf16[24,1280]{1,0:T(8,128)(2,1)S(1)}, bf16[24,1280]{1,0:T(8,128)(2,1)S(1)}, u32[]{:S(2)}, u32[]{:S(2)}) collective-permute-start(bf16[24,1280]{1,0:T(8,128)(2,1)S(1)} %pad_maximum_fusion.21), channel_id=1, source_target_pairs={{0,1},{1,0},{2,3},{3,2},{4,5},{5,4},{6,7},{7,6},{8,9},{9,8},{10,11... | collective-permute-start | bytes 184328 | tf_op jit(solution)/shard_map/ppermute | solution.py:651
  25.0 13.4 %collective-permute-start.2 = (bf16[2,24,1280]{2,1,0:T(8,128)(2,1)S(1)}, bf16[2,24,1280]{2,1,0:T(8,128)(2,1)S(1)}, u32[]{:S(2)}, u32[]{:S(2)}) collective-permute-start(bf16[2,24,1280]{2,1,0:T(8,128)(2,1)S(1)} %pad_maximum_fusion.19), channel_id=1, source_target_pairs={{0,16},{2,18},{4,20},{6,22},{8,24},{10,26},{12,28},{14,30},{16,0},... | collective-permute-start | bytes 368648 | tf_op jit(solution)/shard_map/ppermute | solution.py:651
  38.5 30.0 %copy-start.34 = (s32[1,2]{1,0:T(1,128)S(1)}, s32[1,2]{1,0:T(1,128)}, u32[]{:S(2)}) copy-start(s32[1,2]{1,0:T(1,128)} %param.36) | copy-start | bytes 28
  38.5 33.2 %copy-start.31 = (s32[1,20]{1,0:T(1,128)S(1)}, s32[1,20]{1,0:T(1,128)}, u32[]{:S(2)}) copy-start(s32[1,20]{1,0:T(1,128)} %param.37) | copy-start | bytes 244
  38.6 6.9 %collective-permute-start.3 = (bf16[2,2,24,1280]{3,2,1,0:T(8,128)(2,1)S(1)}, bf16[2,2,24,1280]{3,2,1,0:T(8,128)(2,1)S(1)}, u32[]{:S(2)}, u32[]{:S(2)}) collective-permute-start(bf16[2,2,24,1280]{3,2,1,0:T(8,128)(2,1)S(1)} %pad_maximum_fusion.17), channel_id=1, source_target_pairs={{0,8},{2,10},{4,12},{6,14},{8,0},{10,2},{12,4},{14,6},{16,24},{18,... | collective-permute-start | bytes 737288 | tf_op jit(solution)/shard_map/ppermute | solution.py:651
  45.5 20.9 %collective-permute-start.4 = (bf16[2,2,2,24,1280]{4,3,2,1,0:T(8,128)(2,1)S(1)}, bf16[2,2,2,24,1280]{4,3,2,1,0:T(8,128)(2,1)}, u32[]{:S(2)}, u32[]{:S(2)}) collective-permute-start(bf16[2,2,2,24,1280]{4,3,2,1,0:T(8,128)(2,1)S(1)} %pad_maximum_fusion.14), channel_id=1, source_target_pairs={{0,4},{2,6},{4,0},{6,2},{8,12},{10,14},{12,8},{14,10},{16,20},{18,... | collective-permute-start | bytes 1474568 | tf_op jit(solution)/shard_map/ppermute | solution.py:651
  47.1 44.7 %collective-permute-start = (bf16[1024,768]{1,0:T(8,128)(2,1)S(1)}, bf16[1024,768]{1,0:T(8,128)(2,1)}, u32[]{:S(2)}, u32[]{:S(2)}) collective-permute-start(bf16[1024,768]{1,0:T(8,128)(2,1)S(1)} %copy-done.7), channel_id=1, source_target_pairs={{0,1},{1,0},{2,3},{3,2},{4,5},{5,4},{6,7},{7,6},{8,9},{9,8},{10,11... | collective-permute-start | bytes 4718600 | tf_op jit(solution)/shard_map/ppermute | solution.py:651
  68.5 26.5 %collective-permute-start.5 = (bf16[2,2,2,2,24,1280]{5,4,3,2,1,0:T(8,128)(2,1)}, bf16[2,2,2,2,24,1280]{5,4,3,2,1,0:T(8,128)(2,1)}, u32[]{:S(2)}, u32[]{:S(2)}) collective-permute-start(bf16[2,2,2,2,24,1280]{5,4,3,2,1,0:T(8,128)(2,1)} %pad_maximum_fusion.11), channel_id=1, source_target_pairs={{0,2},{2,0},{4,6},{6,4},{8,10},{10,8},{12,14},{14,12},{16,18},{18,... | collective-permute-start | bytes 2949128 | tf_op jit(solution)/shard_map/ppermute | solution.py:651
  149.5 18.0 %copy-start.2 = (bf16[2048,384]{1,0:T(8,128)(2,1)S(1)}, bf16[2048,384]{1,0:T(8,128)(2,1)}, u32[]{:S(2)}) copy-start(bf16[2048,384]{1,0:T(8,128)(2,1)} %get-tuple-element.27.o_ref) | copy-start | bytes 4718596
  149.5 18.0 %collective-permute-start.6 = (bf16[1024,384]{1,0:T(8,128)(2,1)}, bf16[1024,384]{1,0:T(8,128)(2,1)}, u32[]{:S(2)}, u32[]{:S(2)}) collective-permute-start(bf16[1024,384]{1,0:T(8,128)(2,1)} %broadcast_select_fusion.9), channel_id=1, source_target_pairs={{0,1},{1,0},{2,3},{3,2},{4,5},{5,4},{6,7},{7,6},{8,9},{9,8},{10,11... | collective-permute-start | bytes 2359304 | tf_op jit(solution)/shard_map/ppermute | solution.py:651
  206.8 32.8 %copy-start.26 = (f32[1024]{0:T(1024)}, f32[1024]{0:T(1024)S(1)}, u32[]{:S(2)}) copy-start(f32[1024]{0:T(1024)S(1)} %get-tuple-element.201) | copy-start | bytes 12292
  206.8 32.8 %copy-start.28 = (f32[1024]{0:T(1024)}, f32[1024]{0:T(1024)S(1)}, u32[]{:S(2)}) copy-start(f32[1024]{0:T(1024)S(1)} %get-tuple-element.202) | copy-start | bytes 12292
  254.4 17.0 %collective-permute-start.7 = (bf16[1024,384]{1,0:T(8,128)(2,1)S(1)}, bf16[1024,384]{1,0:T(8,128)(2,1)}, u32[]{:S(2)}, u32[]{:S(2)}) collective-permute-start(bf16[1024,384]{1,0:T(8,128)(2,1)S(1)} %broadcast_select_fusion.5), channel_id=1, source_target_pairs={{0,1},{1,0},{2,3},{3,2},{4,5},{5,4},{6,7},{7,6},{8,9},{9,8},{10,11... | collective-permute-start | bytes 2359304 | tf_op jit(solution)/shard_map/ppermute | solution.py:651
  265.9 80.8 %collective-permute-start.11 = (bf16[8,2,24,896]{3,2,1,0:T(8,128)(2,1)}, bf16[8,2,24,896]{3,2,1,0:T(8,128)(2,1)}, u32[]{:S(2)}, u32[]{:S(2)}) collective-permute-start(bf16[8,2,24,896]{3,2,1,0:T(8,128)(2,1)} %fusion.74), channel_id=1, source_target_pairs={{0,2},{2,0},{4,6},{6,4},{8,10},{10,8},{12,14},{14,12},{16,18},{18,... | collective-permute-start | bytes 2064392 | tf_op jit(solution)/shard_map/ppermute | solution.py:651
  346.6 4.7 %collective-permute-start.9 = (bf16[8,2,24,1280]{3,2,1,0:T(8,128)(2,1)S(1)}, bf16[8,2,24,1280]{3,2,1,0:T(8,128)(2,1)S(1)}, u32[]{:S(2)}, u32[]{:S(2)}) collective-permute-start(bf16[8,2,24,1280]{3,2,1,0:T(8,128)(2,1)S(1)} %fusion.62), channel_id=1, source_target_pairs={{0,2},{2,0},{4,6},{6,4},{8,10},{10,8},{12,14},{14,12},{16,18},{18,... | collective-permute-start | bytes 2949128 | tf_op jit(solution)/shard_map/ppermute | solution.py:651
  348.9 11.5 %collective-permute-start.12 = (bf16[4,2,24,896]{3,2,1,0:T(8,128)(2,1)}, bf16[4,2,24,896]{3,2,1,0:T(8,128)(2,1)}, u32[]{:S(2)}, u32[]{:S(2)}) collective-permute-start(bf16[4,2,24,896]{3,2,1,0:T(8,128)(2,1)} %fusion.79), channel_id=1, source_target_pairs={{0,4},{2,6},{4,0},{6,2},{8,12},{10,14},{12,8},{14,10},{16,20},{18,... | collective-permute-start | bytes 1032200 | tf_op jit(solution)/shard_map/ppermute | solution.py:651
  352.5 20.4 %collective-permute-start.10 = (bf16[4,2,24,1280]{3,2,1,0:T(8,128)(2,1)}, bf16[4,2,24,1280]{3,2,1,0:T(8,128)(2,1)}, u32[]{:S(2)}, u32[]{:S(2)}) collective-permute-start(bf16[4,2,24,1280]{3,2,1,0:T(8,128)(2,1)} %fusion.75), channel_id=1, source_target_pairs={{0,4},{2,6},{4,0},{6,2},{8,12},{10,14},{12,8},{14,10},{16,20},{18,... | collective-permute-start | bytes 1474568 | tf_op jit(solution)/shard_map/ppermute | solution.py:651
  355.6 38.9 %collective-permute-start.8 = (bf16[1024,768]{0,1:T(8,128)(2,1)}, bf16[1024,768]{0,1:T(8,128)(2,1)S(1)}, u32[]{:S(2)}, u32[]{:S(2)}) collective-permute-start(bf16[1024,768]{0,1:T(8,128)(2,1)} %fusion.32), channel_id=1, source_target_pairs={{0,1},{1,0},{2,3},{3,2},{4,5},{5,4},{6,7},{7,6},{8,9},{9,8},{10,11... | collective-permute-start | bytes 4718600 | tf_op jit(solution)/shard_map/ppermute | solution.py:651
  374.5 11.5 %collective-permute-start.13 = (bf16[2,2,24,2176]{3,2,1,0:T(8,128)(2,1)S(1)}, bf16[2,2,24,2176]{3,2,1,0:T(8,128)(2,1)S(1)}, u32[]{:S(2)}, u32[]{:S(2)}) collective-permute-start(bf16[2,2,24,2176]{3,2,1,0:T(8,128)(2,1)S(1)} %fusion.76), channel_id=1, source_target_pairs={{0,8},{2,10},{4,12},{6,14},{8,0},{10,2},{12,4},{14,6},{16,24},{18,... | collective-permute-start | bytes 1253384 | tf_op jit(solution)/shard_map/ppermute | solution.py:651
  388.9 12.7 %collective-permute-start.14 = (bf16[1,2,24,2176]{3,2,1,0:T(8,128)(2,1)}, bf16[1,2,24,2176]{3,2,1,0:T(8,128)(2,1)S(1)}, u32[]{:S(2)}, u32[]{:S(2)}) collective-permute-start(bf16[1,2,24,2176]{3,2,1,0:T(8,128)(2,1)} %fusion.80), channel_id=1, source_target_pairs={{0,16},{2,18},{4,20},{6,22},{8,24},{10,26},{12,28},{14,30},{16,0},... | collective-permute-start | bytes 626696 | tf_op jit(solution)/shard_map/ppermute | solution.py:651
  402.8 4.7 %collective-permute-start.15 = (bf16[24,2176]{1,0:T(8,128)(2,1)S(1)}, bf16[24,2176]{1,0:T(8,128)(2,1)S(1)}, u32[]{:S(2)}, u32[]{:S(2)}) collective-permute-start(bf16[24,2176]{1,0:T(8,128)(2,1)S(1)} %fusion.82), channel_id=1, source_target_pairs={{0,1},{1,0},{2,3},{3,2},{4,5},{5,4},{6,7},{7,6},{8,9},{9,8},{10,11... | collective-permute-start | bytes 313352 | tf_op jit(solution)/shard_map/ppermute | solution.py:651
  (34 other events, 174.1 us)
Sparse Core Ops, SparseCore 0:
  10.9 107.8 all-gather.2
  239.7 138.0 reduce-scatter.1
